TPU v7x, 32 devices: a whole 2x2x4 slice. The times are simulated.
32 devices in a mesh: field: 2 (over core), group: 2 (over y), row: 8 (over z, x).
Axes of the slice: x: 2, y: 2, z: 4, core: 2. Of those that a mesh axis runs over, the one named last changes fastest.
Arguments:
- anomalies: bfloat16 [2, 16384, 512], P('field', ('group', 'row')), may hold values from -6 to 6
- valid_rows: int32 [2, 16], P('field', ('group', 'row')), may hold values from 512 to 1024
- start_basis: float32 [512, 64], replicated, may hold values from -6 to 6
Outputs:
- patterns: float32 [2, 16384, 64], P('field', ('group', 'row'))
- strengths: float32 [64], replicated
Inputs may be any that keep to these rules, and one draw needn't show every extreme that they name: `valid_rows`: the number of ocean points at the head of each shard; the rest of the shard is land and holds values that must be ignored.
All inputs are finite; a program needn't handle non-finite values.
Results may differ from a plain program's by a relative error of at most 0.0003.
Values sent between devices are 32-bit elements; how exact they have to be, the bound alone decides.
No kernel may reach another device: no remote copies, remote signals or barrier semaphores. Data moves between devices by JAX's collectives and lax.ppermute only.
A program may use at most 64 MiB of HBM per device.

v0:
```python
import jax
import jax.numpy as jnp
from jax import lax
from jax.experimental import pallas as pl
from jax.experimental.pallas import tpu as pltpu
from jax.sharding import PartitionSpec as P

HIGH = lax.Precision.HIGHEST
F32 = jnp.float32
BLOCK = 128
TILE = 8
VMEM = pl.BlockSpec(memory_space=pltpu.VMEM)
SMEM = pl.BlockSpec(memory_space=pltpu.SMEM)


def dot(a, b, ca=1, cb=0):
    return lax.dot_general(
        a, b, (((ca,), (cb,)), ((), ())), precision=HIGH, preferred_element_type=F32
    )


def lane_copy(tile, lane):
    return jnp.broadcast_to(tile[:, lane : lane + 1], tile.shape)


def row_copy(tile, row):
    return jnp.broadcast_to(tile[row : row + 1, :], tile.shape)


def iotas(shape):
    return lax.broadcasted_iota(jnp.int32, shape, 0), lax.broadcasted_iota(jnp.int32, shape, 1)


def inverse_factor(tiles):
    tiles = list(tiles)
    steps = len(tiles)
    sub, lane = iotas((TILE, BLOCK))
    cols = [lane_copy(tiles[0], j) for j in range(TILE)]
    out = []
    for s in range(steps):
        k = TILE * s
        tile = tiles[s]
        inside = (lane >= k) & (lane < k + TILE)
        scale, low = [], {}
        for j in range(TILE):
            scale.append(lax.rsqrt(row_copy(cols[j], j)))
            column = cols[j] * scale[j]
            for i in range(j + 1, TILE):
                low[i, j] = row_copy(column, i)
            for c in range(j + 1, TILE):
                cols[c] = cols[c] - column * low[c, j]
        rows = []
        for i in range(TILE):
            row = jnp.where(inside, jnp.where(lane == k + i, 1.0, 0.0), row_copy(tile, i))
            for m in range(i):
                row = row - low[i, m] * rows[m]
            rows.append(row * scale[i])
        new = rows[0]
        for i in range(1, TILE):
            new = jnp.where(sub == i, rows[i], new)
        out.append(jnp.where(lane <= k + sub, new, 0.0))
        for g in range(s + 1, steps):
            t = tiles[g]
            w = []
            for j in range(TILE):
                acc = lane_copy(t, k + j)
                for m in range(j):
                    acc = acc - low[j, m] * w[m]
                w.append(acc * scale[j])
            if g == s + 1:
                cols = [lane_copy(t, k + TILE + c) for c in range(TILE)]
                for c in range(TILE):
                    for i in range(TILE):
                        cols[c] = cols[c] - w[i] * row_copy(w[i], c)
            t = jnp.where(inside, 0.0, t)
            for i in range(TILE):
                t = t - w[i] * rows[i]
            tiles[g] = t
    return out


def layout(nb):
    shared = [(i, i) for i in range(0, nb, 2)]
    return shared + [(i, j) for i in range(nb) for j in range(i + 1, nb)]


def pack(gram, count):
    nb = gram.shape[0] // BLOCK

    def block(i, j):
        return gram[i * BLOCK : (i + 1) * BLOCK, j * BLOCK : (j + 1) * BLOCK]

    row, lane = iotas((BLOCK, BLOCK))
    parts, extra = [], [jnp.full((1, BLOCK), count, F32)]
    for i, j in layout(nb):
        if i == j:
            second = block(i + 1, i + 1)
            parts.append(jnp.where(row <= lane, block(i, i), second))
            extra.append(jnp.sum(jnp.where(row == lane, second, 0.0), axis=0, keepdims=True))
        else:
            parts.append(block(i, j))
    fill = jnp.zeros((-len(extra) % TILE, BLOCK), F32)
    extra = jnp.concatenate(extra + [fill], axis=0)
    parts = jnp.concatenate(parts, axis=0)
    parts = parts.reshape(4, parts.shape[0] // 4, BLOCK)
    return jnp.concatenate([parts, jnp.broadcast_to(extra, (4,) + extra.shape)], axis=1)


def unpack(read, nb, put):
    quarter = nb * nb * BLOCK // 8
    row, lane = iotas((BLOCK, BLOCK))
    inverse = 1.0 / read(0, quarter, 1)

    def block(t):
        halves = []
        for start in (t * BLOCK, t * BLOCK + BLOCK // 2):
            part, offset = divmod(start, quarter)
            halves.append(read(part, offset, BLOCK // 2) * inverse)
        return jnp.concatenate(halves, axis=0)

    for t, (i, j) in enumerate(layout(nb)):
        if i == j:
            both = block(t)
            turned = both.T
            ends = read(0, quarter + 1 + i // 2, 1) * inverse
            put(i, i, jnp.where(row <= lane, both, turned))
            second = jnp.where(row > lane, both, turned)
            put(i + 1, i + 1, jnp.where(row == lane, ends, second))
        else:
            put(i, j, block(t))


def span(i):
    return slice(i * BLOCK, (i + 1) * BLOCK)


def factor_kernel(mine_ref, other_ref, x_ref, y_ref, s_ref, u_ref, d_ref):
    n = x_ref.shape[1]
    nb = n // BLOCK
    own = lax.axis_index("field") == 1

    def read(part, start, rows):
        a = mine_ref[part, start : start + rows, :]
        b = other_ref[part, start : start + rows, :]
        return jnp.where(own, a, b)

    def put(i, j, v):
        s_ref[span(i), span(j)] = v

    unpack(read, nb, put)
    row, lane = iotas((BLOCK, BLOCK))
    for b in range(nb):
        lo, hi = b * BLOCK, (b + 1) * BLOCK
        tiles = [s_ref[lo + r : lo + r + TILE, lo:hi] for r in range(0, BLOCK, TILE)]
        for t, tile in enumerate(inverse_factor(tiles)):
            d_ref[TILE * t : TILE * (t + 1), :] = tile
        u_ref[:, lo:] = dot(d_ref[...], s_ref[lo:hi, lo:])
        for i in range(b + 1, nb):
            a = i * BLOCK
            s_ref[span(i), a:] = s_ref[span(i), a:] - dot(u_ref[:, span(i)], u_ref[:, a:], 0, 0)
        product = dot(x_ref[:, lo:hi], u_ref[:, lo:])
        y_ref[:, lo:] = product if b == 0 else y_ref[:, lo:] + product


def finish_kernel(
    valid_ref, mine_ref, other_ref, y_ref, values_hbm, out_ref, strengths_ref,
    g_ref, values_ref, sem,
):
    copy = pltpu.make_async_copy(values_hbm, values_ref, sem)
    copy.start()
    modes, n = y_ref.shape
    nb = n // BLOCK
    first = lax.axis_index("field") == 0
    for f in range(2):

        def read(part, start, rows, f=f):
            a = mine_ref[part, start : start + rows, :]
            b = other_ref[part, start : start + rows, :]
            return jnp.where(first, a, b) if f == 0 else jnp.where(first, b, a)

        def put(i, j, v, f=f):
            g_ref[f, span(i), span(j)] = v
            if i != j:
                g_ref[f, span(j), span(i)] = v.T

        unpack(read, nb, put)

    def normal(product):
        wide = jnp.concatenate([product, jnp.zeros((modes, BLOCK - modes), F32)], axis=1)
        tiles = [wide[r : r + TILE, :] for r in range(0, modes, TILE)]
        return jnp.concatenate(inverse_factor(tiles), axis=0)[:, :modes]

    y = y_ref[...]
    t = dot(y, g_ref[0])
    inverse = normal(dot(y, t, 1, 1))
    q0 = dot(inverse, y)
    z = dot(inverse, t)
    w = dot(z, g_ref[1])
    inverse = normal(dot(z, w, 1, 1))
    q1 = dot(inverse, z)
    row, lane = iotas((modes, modes))
    diagonal = jnp.sum(jnp.where(row == lane, inverse, 0.0), axis=0, keepdims=True)
    strengths_ref[...] = 1.0 / diagonal
    q = jnp.where(first, q0, q1)
    high = q.astype(jnp.bfloat16)
    low = (q - high.astype(F32)).astype(jnp.bfloat16)
    both = jnp.concatenate([high, low], axis=0)
    copy.wait()
    ocean = valid_ref[0, 0]
    points = values_ref.shape[0]
    step = min(points, 256)
    for r in range(0, points, step):
        product = lax.dot_general(
            both, values_ref[r : r + step, :], (((1,), (1,)), ((), ())),
            preferred_element_type=F32,
        )
        total = product[:modes] + product[modes:]
        _, place = iotas(total.shape)
        out_ref[:, r : r + step] = jnp.where(place + r < ocean, total, 0.0)


AXES = ("field", "group", "row")


def swap(value, which):
    sizes = [lax.axis_size(a) for a in AXES]
    moves = []
    for f in range(sizes[0]):
        axis, b = which(f)
        for g in range(sizes[1]):
            for r in range(sizes[2]):
                there = dict(zip(AXES, (f, g, r)))
                there[axis] ^= 1 << b
                here = (f * sizes[1] + g) * sizes[2] + r
                moves.append(
                    (here, (there["field"] * sizes[1] + there["group"]) * sizes[2] + there["row"])
                )
    return lax.ppermute(value, AXES, moves)


def has_bit(which):
    def of(f):
        axis, b = which(f)
        return (lax.axis_index(axis) >> b) & 1 == 1

    return jnp.where(lax.axis_index("field") == 0, of(0), of(1))


def sum_all(value):
    sizes = {axis: lax.axis_size(axis) for axis in ("row", "group")}
    if any(n & (n - 1) for n in sizes.values()) or min(sizes.values()) < 2:
        return lax.psum(value, ("group", "row"))
    bits = {axis: n.bit_length() - 1 for axis, n in sizes.items()}
    halved = [("row", 0), ("group", 0)]
    whole = [(axis, b) for axis in ("group", "row") for b in range(1, bits[axis])]
    orders = [lambda f, k=k: halved[k ^ f] for k in range(2)]
    turned = whole[1:] + whole[:1]
    for which in orders:
        half = value.shape[0] // 2
        high = has_bit(which)
        keep = jnp.where(high, value[half:], value[:half])
        send = jnp.where(high, value[:half], value[half:])
        value = keep + swap(send, which)
    for pair in zip(whole, turned):
        value = value + swap(value, lambda f, pair=pair: pair[f])
    for which in reversed(orders):
        other = swap(value, which)
        high = has_bit(which)
        value = jnp.concatenate(
            [jnp.where(high, other, value), jnp.where(high, value, other)], axis=0
        )
    return value


def per_device(anomalies, valid_rows, start_basis):
    values = anomalies[0]
    rows_here, n = values.shape
    modes = start_basis.shape[1]
    ocean = valid_rows[0, 0]
    place = lax.broadcasted_iota(jnp.int32, (rows_here, 1), 0)
    masked = jnp.where(place < ocean, values, jnp.zeros_like(values))
    gram = lax.dot_general(
        masked, masked, (((0,), (0,)), ((), ())), preferred_element_type=F32
    )
    mine = sum_all(pack(gram, ocean.astype(F32)))
    other = swap(mine, lambda f: ("field", 0))
    y = pl.pallas_call(
        factor_kernel,
        out_shape=jax.ShapeDtypeStruct((modes, n), F32),
        in_specs=[VMEM, VMEM, VMEM],
        out_specs=VMEM,
        scratch_shapes=[
            pltpu.VMEM((n, n), F32),
            pltpu.VMEM((BLOCK, n), F32),
            pltpu.VMEM((BLOCK, BLOCK), F32),
        ],
    )(mine, other, start_basis.T)
    patterns, strengths = pl.pallas_call(
        finish_kernel,
        out_shape=(
            jax.ShapeDtypeStruct((modes, rows_here), F32),
            jax.ShapeDtypeStruct((1, modes), F32),
        ),
        in_specs=[SMEM, VMEM, VMEM, VMEM, pl.BlockSpec(memory_space=pl.ANY)],
        out_specs=(VMEM, VMEM),
        scratch_shapes=[
            pltpu.VMEM((2, n, n), F32),
            pltpu.VMEM((rows_here, n), jnp.bfloat16),
            pltpu.SemaphoreType.DMA,
        ],
    )(valid_rows, mine, other, y, values)
    return patterns.T[None], strengths[0]


def solution(mesh):
    in_specs = (P("field", ("group", "row"), None), P("field", ("group", "row")), P())
    out_specs = (P("field", ("group", "row"), None), P())
    return jax.shard_map(
        per_device, mesh=mesh, in_specs=in_specs, out_specs=out_specs, check_vma=False
    )
```

profile of v0, /device:TPU:0, one launch (start us, length us, event | category | flops | bytes accessed | tf_op | source)
XLA Modules:
  0.0 67.9 jit_solution(7172514624456541595)
XLA Ops:
  1.3 0.1 pad.9.clone
  1.4 2.6 %fusion = f32[512,512]{1,0:T(8,128)S(1)} fusion(bf16[1,1024,512]{2,1,0:T(8,128)(2,1)} %param.3, pred[1024]{0:T(1024)(128)(4,1)S(1)} %iota_compare_fusion.2), kind=kOutput, calls=%fused_computation | convolution fusion | flops 537395200 | bytes 2098176 | tf_op jit(solution)/shard_map/dot_general | solution.py:282
  4.1 0.1 maximum_maximum_fusion
  4.3 3.0 %collective-permute-start = (f32[2,264,128]{2,1,0:T(8,128)S(1)}, f32[2,264,128]{2,1,0:T(8,128)S(1)}, u32[]{:S(2)}, u32[]{:S(2)}) collective-permute-start(f32[2,264,128]{2,1,0:T(8,128)S(1)} %fusion.6), channel_id=1, source_target_pairs={{0,1},{1,0},{2,3},{3,2},{4,5},{5,4},{6,7},{7,6},{8,9},{9,8},{10,11... | collective-permute-start | bytes 811016 | tf_op jit(solution)/shard_map/ppermute | solution.py:238
  7.3 4.4 %collective-permute-done = f32[2,264,128]{2,1,0:T(8,128)S(1)} collective-permute-done((f32[2,264,128]{2,1,0:T(8,128)S(1)}, f32[2,264,128]{2,1,0:T(8,128)S(1)}, u32[]{:S(2)}, u32[]{:S(2)}) %collective-permute-start) | collective-permute-done | bytes 270368 | tf_op jit(solution)/shard_map/ppermute | solution.py:238
  11.8 2.1 %collective-permute-start.1 = (f32[1,264,128]{2,1,0:T(8,128)S(1)}, f32[1,264,128]{2,1,0:T(8,128)S(1)}, u32[]{:S(2)}, u32[]{:S(2)}) collective-permute-start(f32[1,264,128]{2,1,0:T(8,128)S(1)} %slice_select_fusion), channel_id=1, source_target_pairs={{0,8},{1,9},{2,10},{3,11},{4,12},{5,13},{6,14},{7,15},{8,0},{9,1},... | collective-permute-start | bytes 405512 | tf_op jit(solution)/shard_map/ppermute | solution.py:238
  13.9 3.0 %collective-permute-done.1 = f32[1,264,128]{2,1,0:T(8,128)S(1)} collective-permute-done((f32[1,264,128]{2,1,0:T(8,128)S(1)}, f32[1,264,128]{2,1,0:T(8,128)S(1)}, u32[]{:S(2)}, u32[]{:S(2)}) %collective-permute-start.1) | collective-permute-done | bytes 135200 | tf_op jit(solution)/shard_map/ppermute | solution.py:238
  16.9 2.1 %collective-permute-start.2 = (f32[1,264,128]{2,1,0:T(8,128)S(1)}, f32[1,264,128]{2,1,0:T(8,128)S(1)}, u32[]{:S(2)}, u32[]{:S(2)}) collective-permute-start(f32[1,264,128]{2,1,0:T(8,128)S(1)} %select_add_fusion.1), channel_id=1, source_target_pairs={{0,2},{1,3},{2,0},{3,1},{4,6},{5,7},{6,4},{7,5},{8,10},{9,11},{10,... | collective-permute-start | bytes 405512 | tf_op jit(solution)/shard_map/ppermute | solution.py:238
  19.1 3.3 %collective-permute-done.2 = f32[1,264,128]{2,1,0:T(8,128)S(1)} collective-permute-done((f32[1,264,128]{2,1,0:T(8,128)S(1)}, f32[1,264,128]{2,1,0:T(8,128)S(1)}, u32[]{:S(2)}, u32[]{:S(2)}) %collective-permute-start.2) | collective-permute-done | bytes 135200 | tf_op jit(solution)/shard_map/ppermute | solution.py:238
  22.4 2.8 %collective-permute-start.3 = (f32[1,264,128]{2,1,0:T(8,128)S(1)}, f32[1,264,128]{2,1,0:T(8,128)S(1)}, u32[]{:S(2)}, u32[]{:S(2)}) collective-permute-start(f32[1,264,128]{2,1,0:T(8,128)S(1)} %add.14), channel_id=1, source_target_pairs={{0,4},{1,5},{2,6},{3,7},{4,0},{5,1},{6,2},{7,3},{8,12},{9,13},{10,... | collective-permute-start | bytes 405512 | tf_op jit(solution)/shard_map/ppermute | solution.py:238
  25.2 3.2 %collective-permute-done.3 = f32[1,264,128]{2,1,0:T(8,128)S(1)} collective-permute-done((f32[1,264,128]{2,1,0:T(8,128)S(1)}, f32[1,264,128]{2,1,0:T(8,128)S(1)}, u32[]{:S(2)}, u32[]{:S(2)}) %collective-permute-start.3) | collective-permute-done | bytes 135200 | tf_op jit(solution)/shard_map/ppermute | solution.py:238
  28.4 3.5 %collective-permute-start.4 = (f32[1,264,128]{2,1,0:T(8,128)S(1)}, f32[1,264,128]{2,1,0:T(8,128)S(1)}, u32[]{:S(2)}, u32[]{:S(2)}) collective-permute-start(f32[1,264,128]{2,1,0:T(8,128)S(1)} %add.15), channel_id=1, source_target_pairs={{0,8},{1,9},{2,10},{3,11},{4,12},{5,13},{6,14},{7,15},{8,0},{9,1},... | collective-permute-start | bytes 405512 | tf_op jit(solution)/shard_map/ppermute | solution.py:238
  31.9 4.4 %collective-permute-done.4 = f32[1,264,128]{2,1,0:T(8,128)S(1)} collective-permute-done((f32[1,264,128]{2,1,0:T(8,128)S(1)}, f32[1,264,128]{2,1,0:T(8,128)S(1)}, u32[]{:S(2)}, u32[]{:S(2)}) %collective-permute-start.4) | collective-permute-done | bytes 135200 | tf_op jit(solution)/shard_map/ppermute | solution.py:238
  36.4 2.1 %collective-permute-start.5 = (f32[2,264,128]{2,1,0:T(8,128)S(1)}, f32[2,264,128]{2,1,0:T(8,128)S(1)}, u32[]{:S(2)}, u32[]{:S(2)}) collective-permute-start(f32[2,264,128]{2,1,0:T(8,128)S(1)} %pad_maximum_fusion.2), channel_id=1, source_target_pairs={{0,1},{1,0},{2,3},{3,2},{4,5},{5,4},{6,7},{7,6},{8,9},{9,8},{10,11... | collective-permute-start | bytes 811016 | tf_op jit(solution)/shard_map/ppermute | solution.py:238
  38.5 4.5 %collective-permute-done.5 = f32[2,264,128]{2,1,0:T(8,128)S(1)} collective-permute-done((f32[2,264,128]{2,1,0:T(8,128)S(1)}, f32[2,264,128]{2,1,0:T(8,128)S(1)}, u32[]{:S(2)}, u32[]{:S(2)}) %collective-permute-start.5) | collective-permute-done | bytes 270368 | tf_op jit(solution)/shard_map/ppermute | solution.py:238
  43.0 0.0 copy-start
  43.0 0.1 collective-permute-start.6
  43.1 1.9 %collective-permute-done.6.other_ref = f32[4,264,128]{2,1,0:T(8,128)S(1)} collective-permute-done((f32[4,264,128]{2,1,0:T(8,128)S(1)}, f32[4,264,128]{2,1,0:T(8,128)S(1)}, u32[]{:S(2)}, u32[]{:S(2)}) %collective-permute-start.6) | collective-permute-done | bytes 540704 | tf_op jit(solution)/shard_map/ppermute | solution.py:238
  45.0 0.0 copy-start.1
  45.0 0.0 copy-done
  45.0 0.8 %copy-done.1 = f32[4,264,128]{2,1,0:T(8,128)} copy-done((f32[4,264,128]{2,1,0:T(8,128)}, f32[4,264,128]{2,1,0:T(8,128)S(1)}, u32[]{:S(2)}) %copy-start.1) | copy-done | bytes 540696
  45.8 14.9 %shard_map.50.y_ref = f32[64,512]{1,0:T(8,128)} custom-call(f32[4,264,128]{2,1,0:T(8,128)} %copy-done, f32[4,264,128]{2,1,0:T(8,128)} %copy-done.1, f32[64,512]{1,0:T(8,128)} %bitcast.19), custom_call_target="tpu_custom_call" | custom-call | tf_op jit(solution)/shard_map/pallas_call | solution.py:287
  60.7 7.0 %shard_map.51 = (f32[64,1024]{1,0:T(8,128)}, f32[1,64]{1,0:T(1,128)}) custom-call(s32[1,1]{1,0:T(1,128)} %copy.11.valid_ref, f32[4,264,128]{2,1,0:T(8,128)} %copy-done, f32[4,264,128]{2,1,0:T(8,128)} %copy-done.1, f32[64,512]{1,0:T(8,128)} %shard_map.50.y_ref, bf16[1024,512]{1,0:T(8,128)(2,1)} %bitcast.18), custom_call_target="tpu_custom_call" | custom-call | tf_op jit(solution)/shard_map/pallas_call | solution.py:298
  (21 shorter events, 0.4 us)
Async XLA Ops:
  4.3 7.5 %collective-permute-start = (f32[2,264,128]{2,1,0:T(8,128)S(1)}, f32[2,264,128]{2,1,0:T(8,128)S(1)}, u32[]{:S(2)}, u32[]{:S(2)}) collective-permute-start(f32[2,264,128]{2,1,0:T(8,128)S(1)} %fusion.6), channel_id=1, source_target_pairs={{0,1},{1,0},{2,3},{3,2},{4,5},{5,4},{6,7},{7,6},{8,9},{9,8},{10,11... | collective-permute-start | bytes 811016 | tf_op jit(solution)/shard_map/ppermute | solution.py:238
  11.8 5.1 %collective-permute-start.1 = (f32[1,264,128]{2,1,0:T(8,128)S(1)}, f32[1,264,128]{2,1,0:T(8,128)S(1)}, u32[]{:S(2)}, u32[]{:S(2)}) collective-permute-start(f32[1,264,128]{2,1,0:T(8,128)S(1)} %slice_select_fusion), channel_id=1, source_target_pairs={{0,8},{1,9},{2,10},{3,11},{4,12},{5,13},{6,14},{7,15},{8,0},{9,1},... | collective-permute-start | bytes 405512 | tf_op jit(solution)/shard_map/ppermute | solution.py:238
  16.9 5.4 %collective-permute-start.2 = (f32[1,264,128]{2,1,0:T(8,128)S(1)}, f32[1,264,128]{2,1,0:T(8,128)S(1)}, u32[]{:S(2)}, u32[]{:S(2)}) collective-permute-start(f32[1,264,128]{2,1,0:T(8,128)S(1)} %select_add_fusion.1), channel_id=1, source_target_pairs={{0,2},{1,3},{2,0},{3,1},{4,6},{5,7},{6,4},{7,5},{8,10},{9,11},{10,... | collective-permute-start | bytes 405512 | tf_op jit(solution)/shard_map/ppermute | solution.py:238
  22.4 6.0 %collective-permute-start.3 = (f32[1,264,128]{2,1,0:T(8,128)S(1)}, f32[1,264,128]{2,1,0:T(8,128)S(1)}, u32[]{:S(2)}, u32[]{:S(2)}) collective-permute-start(f32[1,264,128]{2,1,0:T(8,128)S(1)} %add.14), channel_id=1, source_target_pairs={{0,4},{1,5},{2,6},{3,7},{4,0},{5,1},{6,2},{7,3},{8,12},{9,13},{10,... | collective-permute-start | bytes 405512 | tf_op jit(solution)/shard_map/ppermute | solution.py:238
  28.4 7.9 %collective-permute-start.4 = (f32[1,264,128]{2,1,0:T(8,128)S(1)}, f32[1,264,128]{2,1,0:T(8,128)S(1)}, u32[]{:S(2)}, u32[]{:S(2)}) collective-permute-start(f32[1,264,128]{2,1,0:T(8,128)S(1)} %add.15), channel_id=1, source_target_pairs={{0,8},{1,9},{2,10},{3,11},{4,12},{5,13},{6,14},{7,15},{8,0},{9,1},... | collective-permute-start | bytes 405512 | tf_op jit(solution)/shard_map/ppermute | solution.py:238
  36.4 6.5 %collective-permute-start.5 = (f32[2,264,128]{2,1,0:T(8,128)S(1)}, f32[2,264,128]{2,1,0:T(8,128)S(1)}, u32[]{:S(2)}, u32[]{:S(2)}) collective-permute-start(f32[2,264,128]{2,1,0:T(8,128)S(1)} %pad_maximum_fusion.2), channel_id=1, source_target_pairs={{0,1},{1,0},{2,3},{3,2},{4,5},{5,4},{6,7},{7,6},{8,9},{9,8},{10,11... | collective-permute-start | bytes 811016 | tf_op jit(solution)/shard_map/ppermute | solution.py:238
  43.0 2.0 %copy-start = (f32[4,264,128]{2,1,0:T(8,128)}, f32[4,264,128]{2,1,0:T(8,128)S(1)}, u32[]{:S(2)}) copy-start(f32[4,264,128]{2,1,0:T(8,128)S(1)} %pad_maximum_fusion.mine_ref) | copy-start | bytes 1622020
  43.0 2.0 %collective-permute-start.6 = (f32[4,264,128]{2,1,0:T(8,128)S(1)}, f32[4,264,128]{2,1,0:T(8,128)S(1)}, u32[]{:S(2)}, u32[]{:S(2)}) collective-permute-start(f32[4,264,128]{2,1,0:T(8,128)S(1)} %pad_maximum_fusion.mine_ref), channel_id=1, source_target_pairs={{0,16},{1,17},{2,18},{3,19},{4,20},{5,21},{6,22},{7,23},{8,24},{9,... | collective-permute-start | bytes 1622024 | tf_op jit(solution)/shard_map/ppermute | solution.py:238
  45.0 0.8 %copy-start.1 = (f32[4,264,128]{2,1,0:T(8,128)}, f32[4,264,128]{2,1,0:T(8,128)S(1)}, u32[]{:S(2)}) copy-start(f32[4,264,128]{2,1,0:T(8,128)S(1)} %collective-permute-done.6.other_ref) | copy-start | bytes 1622020
where the time goes:
time: 68.1 us; the launch traced here: 67.9 us
  waiting for transfers between devices  24.7 us (36%)
  Pallas kernels  21.9 us (32%)
  starting transfers between devices  15.7 us (23%)
  matrix products  2.59 us (4%)
  between operations  1.57 us (2%)
  local copies, waits for them, and re-layouts  0.94 us (1%)
    ppermute x7, waiting for transfers between devices, swap(): return lax.ppermute(value, AXES, moves)  24.7 us
    ppermute x7, starting transfers between devices, swap(): return lax.ppermute(value, AXES, moves)  15.7 us
    pallas_call x1, Pallas kernels, per_device(): pl.pallas_call(factor_kernel, out_shape=jax.ShapeDtypeStruct((modes, n),...  14.9 us
    pallas_call x1, Pallas kernels, per_device(): pl.pallas_call(finish_kernel, out_shape=(jax.ShapeDtypeStruct((modes, row...  7 us
    dot_general x1, matrix products, per_device(): lax.dot_general(masked, masked, (((0,), (0,)), ((), ())), preferred_eleme...  2.59 us
  transfers between devices with their start and end apart: 7, of which 7 were waited for; matrix products, arithmetic and copies ran while one was open for 0% of the time, Pallas kernels for 0%

commit v1 on v0

--- a/solution.py
+++ b/solution.py
@@ -9,6 +9,7 @@
 F32 = jnp.float32
 BLOCK = 128
 TILE = 8
+GRANT = 16 * 2**20
 VMEM = pl.BlockSpec(memory_space=pltpu.VMEM)
 SMEM = pl.BlockSpec(memory_space=pltpu.SMEM)
 
@@ -134,21 +135,31 @@
     return slice(i * BLOCK, (i + 1) * BLOCK)
 
 
-def factor_kernel(mine_ref, other_ref, x_ref, y_ref, s_ref, u_ref, d_ref):
+def factor_kernel(part_ref, rest_ref, x_ref, y_ref, s_ref, u_ref, d_ref):
+    @pl.when(lax.axis_index("field") == 0)
+    def _():
+        y_ref[...] = jnp.zeros_like(y_ref)
+
+    @pl.when(lax.axis_index("field") == 1)
+    def _():
+        apply_factor(part_ref, rest_ref, x_ref, y_ref, s_ref, u_ref, d_ref)
+
+
+def apply_factor(part_ref, rest_ref, x_ref, y_ref, s_ref, u_ref, d_ref):
     n = x_ref.shape[1]
     nb = n // BLOCK
-    own = lax.axis_index("field") == 1
+    half = part_ref.shape[0]
+    high = has_bit(bit_orders()[0])
 
     def read(part, start, rows):
-        a = mine_ref[part, start : start + rows, :]
-        b = other_ref[part, start : start + rows, :]
-        return jnp.where(own, a, b)
+        a = part_ref[part % half, start : start + rows, :]
+        b = rest_ref[part % half, start : start + rows, :]
+        return jnp.where(high, a, b) if part >= half else jnp.where(high, b, a)
 
     def put(i, j, v):
         s_ref[span(i), span(j)] = v
 
     unpack(read, nb, put)
-    row, lane = iotas((BLOCK, BLOCK))
     for b in range(nb):
         lo, hi = b * BLOCK, (b + 1) * BLOCK
         tiles = [s_ref[lo + r : lo + r + TILE, lo:hi] for r in range(0, BLOCK, TILE)]
@@ -163,7 +174,7 @@
 
 
 def finish_kernel(
-    valid_ref, mine_ref, other_ref, y_ref, values_hbm, out_ref, strengths_ref,
+    valid_ref, mine_ref, other_ref, y_ref, y_other_ref, values_hbm, out_ref, strengths_ref,
     g_ref, values_ref, sem,
 ):
     copy = pltpu.make_async_copy(values_hbm, values_ref, sem)
@@ -190,7 +201,7 @@
         tiles = [wide[r : r + TILE, :] for r in range(0, modes, TILE)]
         return jnp.concatenate(inverse_factor(tiles), axis=0)[:, :modes]
 
-    y = y_ref[...]
+    y = jnp.where(first, y_other_ref[...], y_ref[...])
     t = dot(y, g_ref[0])
     inverse = normal(dot(y, t, 1, 1))
     q0 = dot(inverse, y)
@@ -246,30 +257,32 @@
     return jnp.where(lax.axis_index("field") == 0, of(0), of(1))
 
 
+def bit_orders():
+    sizes = {axis: lax.axis_size(axis) for axis in ("row", "group")}
+    bits = {axis: n.bit_length() - 1 for axis, n in sizes.items()}
+    order = [("row", 0), ("group", 0)]
+    order += [(axis, b) for axis in ("row", "group") for b in range(1, bits[axis])]
+    return [lambda f, k=k: order[(k + 2 * (1 - f)) % len(order)] for k in range(len(order))]
+
+
+def joined(high, value, other):
+    return jnp.concatenate(
+        [jnp.where(high, other, value), jnp.where(high, value, other)], axis=0
+    )
+
+
 def sum_all(value):
-    sizes = {axis: lax.axis_size(axis) for axis in ("row", "group")}
-    if any(n & (n - 1) for n in sizes.values()) or min(sizes.values()) < 2:
-        return lax.psum(value, ("group", "row"))
-    bits = {axis: n.bit_length() - 1 for axis, n in sizes.items()}
-    halved = [("row", 0), ("group", 0)]
-    whole = [(axis, b) for axis in ("group", "row") for b in range(1, bits[axis])]
-    orders = [lambda f, k=k: halved[k ^ f] for k in range(2)]
-    turned = whole[1:] + whole[:1]
-    for which in orders:
+    orders = bit_orders()
+    for which in orders[:2]:
         half = value.shape[0] // 2
         high = has_bit(which)
         keep = jnp.where(high, value[half:], value[:half])
         send = jnp.where(high, value[:half], value[half:])
         value = keep + swap(send, which)
-    for pair in zip(whole, turned):
-        value = value + swap(value, lambda f, pair=pair: pair[f])
-    for which in reversed(orders):
-        other = swap(value, which)
-        high = has_bit(which)
-        value = jnp.concatenate(
-            [jnp.where(high, other, value), jnp.where(high, value, other)], axis=0
-        )
-    return value
+    for which in orders[2:]:
+        value = value + swap(value, which)
+    value = joined(has_bit(orders[1]), value, swap(value, orders[1]))
+    return value, swap(value, orders[0])
 
 
 def per_device(anomalies, valid_rows, start_basis):
@@ -282,8 +295,8 @@
     gram = lax.dot_general(
         masked, masked, (((0,), (0,)), ((), ())), preferred_element_type=F32
     )
-    mine = sum_all(pack(gram, ocean.astype(F32)))
-    other = swap(mine, lambda f: ("field", 0))
+    part, rest = sum_all(pack(gram, ocean.astype(F32)))
+    mine = joined(has_bit(bit_orders()[0]), part, rest)
     y = pl.pallas_call(
         factor_kernel,
         out_shape=jax.ShapeDtypeStruct((modes, n), F32),
@@ -294,21 +307,27 @@
             pltpu.VMEM((BLOCK, n), F32),
             pltpu.VMEM((BLOCK, BLOCK), F32),
         ],
-    )(mine, other, start_basis.T)
+        compiler_params=pltpu.CompilerParams(vmem_limit_bytes=GRANT),
+    )(part, rest, start_basis.T)
+    y, mine = lax.optimization_barrier((y, mine))
+    partner = lambda f: ("field", 0)
+    y_other = swap(y, partner)
+    other = swap(mine, partner)
     patterns, strengths = pl.pallas_call(
         finish_kernel,
         out_shape=(
             jax.ShapeDtypeStruct((modes, rows_here), F32),
             jax.ShapeDtypeStruct((1, modes), F32),
         ),
-        in_specs=[SMEM, VMEM, VMEM, VMEM, pl.BlockSpec(memory_space=pl.ANY)],
+        in_specs=[SMEM, VMEM, VMEM, VMEM, VMEM, pl.BlockSpec(memory_space=pl.ANY)],
         out_specs=(VMEM, VMEM),
         scratch_shapes=[
             pltpu.VMEM((2, n, n), F32),
             pltpu.VMEM((rows_here, n), jnp.bfloat16),
             pltpu.SemaphoreType.DMA,
         ],
-    )(valid_rows, mine, other, y, values)
+        compiler_params=pltpu.CompilerParams(vmem_limit_bytes=GRANT),
+    )(valid_rows, mine, other, y, y_other, values)
     return patterns.T[None], strengths[0]
 
 

time: 68.1 us -> 58 us (0.85)
  Pallas kernels: 21.9 us -> 6.05 us
  starting transfers between devices: 15.7 us -> 20.2 us
    pallas_call x1, Pallas kernels: 14.9 us -> 0.19 us  [per_device(): pl.pallas_call(factor_kernel, out_shape=jax.ShapeDtypeStruct((modes, n),...]
    ppermute x7 -> x8, starting transfers between devices: 15.7 us -> 20.2 us  [swap(): return lax.ppermute(value, AXES, moves)]
    pallas_call x1, Pallas kernels: 7 us -> 5.86 us  [per_device(): pl.pallas_call(finish_kernel, out_shape=(jax.ShapeDtypeStruct((modes, row...]
    ppermute x7 -> x8, waiting for transfers between devices: 24.7 us -> 25.2 us  [swap(): return lax.ppermute(value, AXES, moves)]
  transfers between devices with their start and end apart: 7 -> 8, of which waited for: 7 -> 7; matrix products, arithmetic and copies ran while one was open for 0% -> 0% of each run, Pallas kernels for 0% -> 0%
where the time goes in v1:
time: 58 us; the launch traced here: 57.1 us
  waiting for transfers between devices  25.2 us (43%)
  starting transfers between devices  20.2 us (35%)
  Pallas kernels  6.05 us (10%)
  matrix products  2.67 us (5%)
  between operations  1.58 us (3%)
  local copies, waits for them, and re-layouts  0.95 us (2%)
    ppermute x8, waiting for transfers between devices, swap(): return lax.ppermute(value, AXES, moves)  25.2 us
    ppermute x8, starting transfers between devices, swap(): return lax.ppermute(value, AXES, moves)  20.2 us
    pallas_call x1, Pallas kernels, per_device(): pl.pallas_call(finish_kernel, out_shape=(jax.ShapeDtypeStruct((modes, row...  5.86 us
    dot_general x1, matrix products, per_device(): lax.dot_general(masked, masked, (((0,), (0,)), ((), ())), preferred_eleme...  2.67 us
  transfers between devices with their start and end apart: 8, of which 7 were waited for; matrix products, arithmetic and copies ran while one was open for 0% of the time, Pallas kernels for 0%

profile of v1, /device:TPU:0, one launch (start us, length us, event | category | flops | bytes accessed | tf_op | source)
XLA Modules:
  0.0 57.1 jit_solution(8154292042504581103)
XLA Ops:
  1.3 0.1 pad.9.clone
  1.4 2.7 %fusion = f32[512,512]{1,0:T(8,128)S(1)} fusion(bf16[1,1024,512]{2,1,0:T(8,128)(2,1)} %param.3, pred[1024]{0:T(1024)(128)(4,1)S(1)} %iota_compare_fusion.2), kind=kOutput, calls=%fused_computation | convolution fusion | flops 537395200 | bytes 2098176 | tf_op jit(solution)/shard_map/dot_general | solution.py:295
  4.2 0.1 maximum_maximum_fusion
  4.3 3.1 %collective-permute-start = (f32[2,264,128]{2,1,0:T(8,128)S(1)}, f32[2,264,128]{2,1,0:T(8,128)S(1)}, u32[]{:S(2)}, u32[]{:S(2)}) collective-permute-start(f32[2,264,128]{2,1,0:T(8,128)S(1)} %fusion.6), channel_id=1, source_target_pairs={{0,2},{1,3},{2,0},{3,1},{4,6},{5,7},{6,4},{7,5},{8,10},{9,11},{10,... | collective-permute-start | bytes 811016 | tf_op jit(solution)/shard_map/ppermute | solution.py:249
  7.5 4.4 %collective-permute-done = f32[2,264,128]{2,1,0:T(8,128)S(1)} collective-permute-done((f32[2,264,128]{2,1,0:T(8,128)S(1)}, f32[2,264,128]{2,1,0:T(8,128)S(1)}, u32[]{:S(2)}, u32[]{:S(2)}) %collective-permute-start) | collective-permute-done | bytes 270368 | tf_op jit(solution)/shard_map/ppermute | solution.py:249
  12.0 3.1 %collective-permute-start.1 = (f32[1,264,128]{2,1,0:T(8,128)S(1)}, f32[1,264,128]{2,1,0:T(8,128)S(1)}, u32[]{:S(2)}, u32[]{:S(2)}) collective-permute-start(f32[1,264,128]{2,1,0:T(8,128)S(1)} %slice_select_fusion), channel_id=1, source_target_pairs={{0,4},{1,5},{2,6},{3,7},{4,0},{5,1},{6,2},{7,3},{8,12},{9,13},{10,... | collective-permute-start | bytes 405512 | tf_op jit(solution)/shard_map/ppermute | solution.py:249
  15.1 4.4 %collective-permute-done.1 = f32[1,264,128]{2,1,0:T(8,128)S(1)} collective-permute-done((f32[1,264,128]{2,1,0:T(8,128)S(1)}, f32[1,264,128]{2,1,0:T(8,128)S(1)}, u32[]{:S(2)}, u32[]{:S(2)}) %collective-permute-start.1) | collective-permute-done | bytes 135200 | tf_op jit(solution)/shard_map/ppermute | solution.py:249
  19.5 1.9 %collective-permute-start.2 = (f32[1,264,128]{2,1,0:T(8,128)S(1)}, f32[1,264,128]{2,1,0:T(8,128)S(1)}, u32[]{:S(2)}, u32[]{:S(2)}) collective-permute-start(f32[1,264,128]{2,1,0:T(8,128)S(1)} %select_add_fusion.1), channel_id=1, source_target_pairs={{0,1},{1,0},{2,3},{3,2},{4,5},{5,4},{6,7},{7,6},{8,9},{9,8},{10,11... | collective-permute-start | bytes 405512 | tf_op jit(solution)/shard_map/ppermute | solution.py:249
  21.4 3.2 %collective-permute-done.2 = f32[1,264,128]{2,1,0:T(8,128)S(1)} collective-permute-done((f32[1,264,128]{2,1,0:T(8,128)S(1)}, f32[1,264,128]{2,1,0:T(8,128)S(1)}, u32[]{:S(2)}, u32[]{:S(2)}) %collective-permute-start.2) | collective-permute-done | bytes 135200 | tf_op jit(solution)/shard_map/ppermute | solution.py:249
  24.6 1.9 %collective-permute-start.3 = (f32[1,264,128]{2,1,0:T(8,128)S(1)}, f32[1,264,128]{2,1,0:T(8,128)S(1)}, u32[]{:S(2)}, u32[]{:S(2)}) collective-permute-start(f32[1,264,128]{2,1,0:T(8,128)S(1)} %add.14), channel_id=1, source_target_pairs={{0,8},{1,9},{2,10},{3,11},{4,12},{5,13},{6,14},{7,15},{8,0},{9,1},... | collective-permute-start | bytes 405512 | tf_op jit(solution)/shard_map/ppermute | solution.py:249
  26.6 3.8 %collective-permute-done.3 = f32[1,264,128]{2,1,0:T(8,128)S(1)} collective-permute-done((f32[1,264,128]{2,1,0:T(8,128)S(1)}, f32[1,264,128]{2,1,0:T(8,128)S(1)}, u32[]{:S(2)}, u32[]{:S(2)}) %collective-permute-start.3) | collective-permute-done | bytes 135200 | tf_op jit(solution)/shard_map/ppermute | solution.py:249
  30.4 2.8 %collective-permute-start.4 = (f32[1,264,128]{2,1,0:T(8,128)S(1)}, f32[1,264,128]{2,1,0:T(8,128)S(1)}, u32[]{:S(2)}, u32[]{:S(2)}) collective-permute-start(f32[1,264,128]{2,1,0:T(8,128)S(1)} %add.15), channel_id=1, source_target_pairs={{0,4},{1,5},{2,6},{3,7},{4,0},{5,1},{6,2},{7,3},{8,12},{9,13},{10,... | collective-permute-start | bytes 405512 | tf_op jit(solution)/shard_map/ppermute | solution.py:249
  33.2 3.2 %collective-permute-done.4 = f32[1,264,128]{2,1,0:T(8,128)S(1)} collective-permute-done((f32[1,264,128]{2,1,0:T(8,128)S(1)}, f32[1,264,128]{2,1,0:T(8,128)S(1)}, u32[]{:S(2)}, u32[]{:S(2)}) %collective-permute-start.4) | collective-permute-done | bytes 135200 | tf_op jit(solution)/shard_map/ppermute | solution.py:249
  36.4 2.3 %collective-permute-start.5 = (f32[2,264,128]{2,1,0:T(8,128)S(1)}, f32[2,264,128]{2,1,0:T(8,128)S(1)}, u32[]{:S(2)}, u32[]{:S(2)}) collective-permute-start(f32[2,264,128]{2,1,0:T(8,128)S(1)} %pad_maximum_fusion.2.part_ref), channel_id=1, source_target_pairs={{0,2},{1,3},{2,0},{3,1},{4,6},{5,7},{6,4},{7,5},{8,10},{9,11},{10,... | collective-permute-start | bytes 811016 | tf_op jit(solution)/shard_map/ppermute | solution.py:249
  38.7 4.4 %collective-permute-done.5.rest_ref = f32[2,264,128]{2,1,0:T(8,128)S(1)} collective-permute-done((f32[2,264,128]{2,1,0:T(8,128)S(1)}, f32[2,264,128]{2,1,0:T(8,128)S(1)}, u32[]{:S(2)}, u32[]{:S(2)}) %collective-permute-start.5) | collective-permute-done | bytes 270368 | tf_op jit(solution)/shard_map/ppermute | solution.py:249
  43.2 0.0 copy-start
  43.3 0.8 %copy-done.1 = f32[512,64]{0,1:T(8,128)S(1)} copy-done((f32[512,64]{0,1:T(8,128)S(1)}, f32[512,64]{0,1:T(8,128)}, u32[]{:S(2)}) %copy-start.1) | copy-done | bytes 131096
  44.1 0.2 shard_map.50.y_ref
  44.3 5.1 %collective-permute-start.6 = (f32[4,264,128]{2,1,0:T(8,128)S(1)}, f32[4,264,128]{2,1,0:T(8,128)S(1)}, u32[]{:S(2)}, u32[]{:S(2)}) collective-permute-start(f32[4,264,128]{2,1,0:T(8,128)S(1)} %pad_maximum_fusion.mine_ref), channel_id=1, source_target_pairs={{0,16},{1,17},{2,18},{3,19},{4,20},{5,21},{6,22},{7,23},{8,24},{9,... | collective-permute-start | bytes 1622024 | tf_op jit(solution)/shard_map/ppermute | solution.py:249
  49.3 0.1 collective-permute-start.7
  49.4 1.7 %collective-permute-done.7.y_other_ref = f32[64,512]{1,0:T(8,128)S(1)} collective-permute-done((f32[64,512]{1,0:T(8,128)S(1)}, f32[64,512]{1,0:T(8,128)S(1)}, u32[]{:S(2)}, u32[]{:S(2)}) %collective-permute-start.7) | collective-permute-done | bytes 131104 | tf_op jit(solution)/shard_map/ppermute | solution.py:249
  51.1 0.0 collective-permute-done.6.other_ref
  51.1 0.0 copy-done
  51.1 5.9 %shard_map.51 = (f32[64,1024]{1,0:T(8,128)}, f32[1,64]{1,0:T(1,128)}) custom-call(s32[1,1]{1,0:T(1,128)} %copy.11.valid_ref, f32[4,264,128]{2,1,0:T(8,128)S(1)} %pad_maximum_fusion.mine_ref, f32[4,264,128]{2,1,0:T(8,128)S(1)} %collective-permute-done.6.other_ref, f32[64,512]{1,0:T(8,128)S(1)} %shard_map.50.y_ref, ...), custom_call_target="tpu_custom_call" | custom-call | tf_op jit(solution)/shard_map/pallas_call | solution.py:316
  (22 shorter events, 0.4 us)
Async XLA Ops:
  4.3 7.6 %collective-permute-start = (f32[2,264,128]{2,1,0:T(8,128)S(1)}, f32[2,264,128]{2,1,0:T(8,128)S(1)}, u32[]{:S(2)}, u32[]{:S(2)}) collective-permute-start(f32[2,264,128]{2,1,0:T(8,128)S(1)} %fusion.6), channel_id=1, source_target_pairs={{0,2},{1,3},{2,0},{3,1},{4,6},{5,7},{6,4},{7,5},{8,10},{9,11},{10,... | collective-permute-start | bytes 811016 | tf_op jit(solution)/shard_map/ppermute | solution.py:249
  12.0 7.5 %collective-permute-start.1 = (f32[1,264,128]{2,1,0:T(8,128)S(1)}, f32[1,264,128]{2,1,0:T(8,128)S(1)}, u32[]{:S(2)}, u32[]{:S(2)}) collective-permute-start(f32[1,264,128]{2,1,0:T(8,128)S(1)} %slice_select_fusion), channel_id=1, source_target_pairs={{0,4},{1,5},{2,6},{3,7},{4,0},{5,1},{6,2},{7,3},{8,12},{9,13},{10,... | collective-permute-start | bytes 405512 | tf_op jit(solution)/shard_map/ppermute | solution.py:249
  19.5 5.1 %collective-permute-start.2 = (f32[1,264,128]{2,1,0:T(8,128)S(1)}, f32[1,264,128]{2,1,0:T(8,128)S(1)}, u32[]{:S(2)}, u32[]{:S(2)}) collective-permute-start(f32[1,264,128]{2,1,0:T(8,128)S(1)} %select_add_fusion.1), channel_id=1, source_target_pairs={{0,1},{1,0},{2,3},{3,2},{4,5},{5,4},{6,7},{7,6},{8,9},{9,8},{10,11... | collective-permute-start | bytes 405512 | tf_op jit(solution)/shard_map/ppermute | solution.py:249
  24.6 5.7 %collective-permute-start.3 = (f32[1,264,128]{2,1,0:T(8,128)S(1)}, f32[1,264,128]{2,1,0:T(8,128)S(1)}, u32[]{:S(2)}, u32[]{:S(2)}) collective-permute-start(f32[1,264,128]{2,1,0:T(8,128)S(1)} %add.14), channel_id=1, source_target_pairs={{0,8},{1,9},{2,10},{3,11},{4,12},{5,13},{6,14},{7,15},{8,0},{9,1},... | collective-permute-start | bytes 405512 | tf_op jit(solution)/shard_map/ppermute | solution.py:249
  30.4 6.0 %collective-permute-start.4 = (f32[1,264,128]{2,1,0:T(8,128)S(1)}, f32[1,264,128]{2,1,0:T(8,128)S(1)}, u32[]{:S(2)}, u32[]{:S(2)}) collective-permute-start(f32[1,264,128]{2,1,0:T(8,128)S(1)} %add.15), channel_id=1, source_target_pairs={{0,4},{1,5},{2,6},{3,7},{4,0},{5,1},{6,2},{7,3},{8,12},{9,13},{10,... | collective-permute-start | bytes 405512 | tf_op jit(solution)/shard_map/ppermute | solution.py:249
  36.4 6.7 %collective-permute-start.5 = (f32[2,264,128]{2,1,0:T(8,128)S(1)}, f32[2,264,128]{2,1,0:T(8,128)S(1)}, u32[]{:S(2)}, u32[]{:S(2)}) collective-permute-start(f32[2,264,128]{2,1,0:T(8,128)S(1)} %pad_maximum_fusion.2.part_ref), channel_id=1, source_target_pairs={{0,2},{1,3},{2,0},{3,1},{4,6},{5,7},{6,4},{7,5},{8,10},{9,11},{10,... | collective-permute-start | bytes 811016 | tf_op jit(solution)/shard_map/ppermute | solution.py:249
  43.2 0.9 %copy-start.1 = (f32[512,64]{0,1:T(8,128)S(1)}, f32[512,64]{0,1:T(8,128)}, u32[]{:S(2)}) copy-start(f32[512,64]{0,1:T(8,128)} %param.5) | copy-start | bytes 393220
  43.2 7.9 %copy-start = (bf16[1,1024,512]{2,1,0:T(8,128)(2,1)S(1)}, bf16[1,1024,512]{2,1,0:T(8,128)(2,1)}, u32[]{:S(2)}) copy-start(bf16[1,1024,512]{2,1,0:T(8,128)(2,1)} %param.3) | copy-start | bytes 3145732
  44.3 6.8 %collective-permute-start.6 = (f32[4,264,128]{2,1,0:T(8,128)S(1)}, f32[4,264,128]{2,1,0:T(8,128)S(1)}, u32[]{:S(2)}, u32[]{:S(2)}) collective-permute-start(f32[4,264,128]{2,1,0:T(8,128)S(1)} %pad_maximum_fusion.mine_ref), channel_id=1, source_target_pairs={{0,16},{1,17},{2,18},{3,19},{4,20},{5,21},{6,22},{7,23},{8,24},{9,... | collective-permute-start | bytes 1622024 | tf_op jit(solution)/shard_map/ppermute | solution.py:249
  49.3 1.7 %collective-permute-start.7 = (f32[64,512]{1,0:T(8,128)S(1)}, f32[64,512]{1,0:T(8,128)S(1)}, u32[]{:S(2)}, u32[]{:S(2)}) collective-permute-start(f32[64,512]{1,0:T(8,128)S(1)} %shard_map.50.y_ref), channel_id=1, source_target_pairs={{0,16},{1,17},{2,18},{3,19},{4,20},{5,21},{6,22},{7,23},{8,24},{9,... | collective-permute-start | bytes 393224 | tf_op jit(solution)/shard_map/ppermute | solution.py:249

commit v2 on v1

--- a/solution.py
+++ b/solution.py
@@ -9,6 +9,7 @@
 F32 = jnp.float32
 BLOCK = 128
 TILE = 8
+HALF = 64
 GRANT = 16 * 2**20
 VMEM = pl.BlockSpec(memory_space=pltpu.VMEM)
 SMEM = pl.BlockSpec(memory_space=pltpu.SMEM)
@@ -20,6 +21,24 @@
     )
 
 
+def thirds(x):
+    high = x.astype(jnp.bfloat16)
+    rest = x - high.astype(F32)
+    middle = rest.astype(jnp.bfloat16)
+    return high, middle, (rest - middle.astype(F32)).astype(jnp.bfloat16)
+
+
+def stacked(a, b, dim=0):
+    ah, am, al = thirds(a)
+    bh, bm, bl = thirds(b)
+    return lax.dot_general(
+        jnp.concatenate([ah, ah, am, ah, al, am], axis=dim),
+        jnp.concatenate([bh, bm, bh, bl, bh, bm], axis=0),
+        (((dim,), (0,)), ((), ())),
+        preferred_element_type=F32,
+    )
+
+
 def lane_copy(tile, lane):
     return jnp.broadcast_to(tile[:, lane : lane + 1], tile.shape)
 
@@ -32,14 +51,14 @@
     return lax.broadcasted_iota(jnp.int32, shape, 0), lax.broadcasted_iota(jnp.int32, shape, 1)
 
 
-def inverse_factor(tiles):
+def eliminate(tiles, base):
     tiles = list(tiles)
     steps = len(tiles)
     sub, lane = iotas((TILE, BLOCK))
-    cols = [lane_copy(tiles[0], j) for j in range(TILE)]
+    cols = [lane_copy(tiles[0], base + j) for j in range(TILE)]
     out = []
     for s in range(steps):
-        k = TILE * s
+        k = base + TILE * s
         tile = tiles[s]
         inside = (lane >= k) & (lane < k + TILE)
         scale, low = [], {}
@@ -59,7 +78,7 @@
         new = rows[0]
         for i in range(1, TILE):
             new = jnp.where(sub == i, rows[i], new)
-        out.append(jnp.where(lane <= k + sub, new, 0.0))
+        out.append(new)
         for g in range(s + 1, steps):
             t = tiles[g]
             w = []
@@ -80,6 +99,28 @@
     return out
 
 
+def inverse_factor(tiles, size):
+    tiles = list(tiles)
+    out = []
+    count = size // TILE
+    _, lane = iotas((TILE, BLOCK))
+    for base in range(0, len(tiles) * TILE, size):
+        done = eliminate(tiles[:count], base)
+        out += done
+        tiles = tiles[count:]
+        if tiles:
+            rows = jnp.concatenate(done, axis=0)
+            place, at = iotas(rows.shape)
+            keep = (at <= place + base) | (at >= base + size)
+            update = stacked(rows, jnp.where(keep, rows, 0.0))
+            for g in range(len(tiles)):
+                start = base + size + TILE * g
+                kept = jnp.where(lane < base + size, jnp.where(lane < base, tiles[g], 0.0), tiles[g])
+                tiles[g] = kept - update[start : start + TILE, :]
+    sub, _ = iotas((TILE, BLOCK))
+    return [jnp.where(lane <= TILE * s + sub, t, 0.0) for s, t in enumerate(out)]
+
+
 def layout(nb):
     shared = [(i, i) for i in range(0, nb, 2)]
     return shared + [(i, j) for i in range(nb) for j in range(i + 1, nb)]
@@ -135,17 +176,19 @@
     return slice(i * BLOCK, (i + 1) * BLOCK)
 
 
-def factor_kernel(part_ref, rest_ref, x_ref, y_ref, s_ref, u_ref, d_ref):
+def factor_kernel(part_ref, rest_ref, x_hbm, y_ref, s_ref, u_ref, x_ref, sem):
     @pl.when(lax.axis_index("field") == 0)
     def _():
         y_ref[...] = jnp.zeros_like(y_ref)
 
     @pl.when(lax.axis_index("field") == 1)
     def _():
-        apply_factor(part_ref, rest_ref, x_ref, y_ref, s_ref, u_ref, d_ref)
-
-
-def apply_factor(part_ref, rest_ref, x_ref, y_ref, s_ref, u_ref, d_ref):
+        apply_factor(part_ref, rest_ref, x_hbm, y_ref, s_ref, u_ref, x_ref, sem)
+
+
+def apply_factor(part_ref, rest_ref, x_hbm, y_ref, s_ref, u_ref, x_ref, sem):
+    copy = pltpu.make_async_copy(x_hbm, x_ref, sem)
+    copy.start()
     n = x_ref.shape[1]
     nb = n // BLOCK
     half = part_ref.shape[0]
@@ -163,12 +206,19 @@
     for b in range(nb):
         lo, hi = b * BLOCK, (b + 1) * BLOCK
         tiles = [s_ref[lo + r : lo + r + TILE, lo:hi] for r in range(0, BLOCK, TILE)]
-        for t, tile in enumerate(inverse_factor(tiles)):
-            d_ref[TILE * t : TILE * (t + 1), :] = tile
-        u_ref[:, lo:] = dot(d_ref[...], s_ref[lo:hi, lo:])
-        for i in range(b + 1, nb):
-            a = i * BLOCK
-            s_ref[span(i), a:] = s_ref[span(i), a:] - dot(u_ref[:, span(i)], u_ref[:, a:], 0, 0)
+        inverse = jnp.concatenate(inverse_factor(tiles, HALF), axis=0)
+        if hi < n:
+            near = stacked(inverse, s_ref[lo:hi, hi : hi + BLOCK], 1)
+            u_ref[:, hi : hi + BLOCK] = near
+            s_ref[span(b + 1), hi : hi + BLOCK] -= stacked(near, near)
+        if hi + BLOCK < n:
+            u_ref[:, hi + BLOCK :] = stacked(inverse, s_ref[lo:hi, hi + BLOCK :], 1)
+            s_ref[span(b + 1), hi + BLOCK :] -= stacked(near, u_ref[:, hi + BLOCK :])
+        u_ref[:, lo:hi] = stacked(inverse, s_ref[lo:hi, lo:hi], 1)
+        for i in range(b + 2, nb):
+            s_ref[span(i), i * BLOCK :] -= stacked(u_ref[:, span(i)], u_ref[:, i * BLOCK :])
+        if b == 0:
+            copy.wait()
         product = dot(x_ref[:, lo:hi], u_ref[:, lo:])
         y_ref[:, lo:] = product if b == 0 else y_ref[:, lo:] + product
 
@@ -199,7 +249,7 @@
     def normal(product):
         wide = jnp.concatenate([product, jnp.zeros((modes, BLOCK - modes), F32)], axis=1)
         tiles = [wide[r : r + TILE, :] for r in range(0, modes, TILE)]
-        return jnp.concatenate(inverse_factor(tiles), axis=0)[:, :modes]
+        return jnp.concatenate(inverse_factor(tiles, modes), axis=0)[:, :modes]
 
     y = jnp.where(first, y_other_ref[...], y_ref[...])
     t = dot(y, g_ref[0])
@@ -300,12 +350,13 @@
     y = pl.pallas_call(
         factor_kernel,
         out_shape=jax.ShapeDtypeStruct((modes, n), F32),
-        in_specs=[VMEM, VMEM, VMEM],
+        in_specs=[VMEM, VMEM, pl.BlockSpec(memory_space=pltpu.HBM)],
         out_specs=VMEM,
         scratch_shapes=[
             pltpu.VMEM((n, n), F32),
             pltpu.VMEM((BLOCK, n), F32),
-            pltpu.VMEM((BLOCK, BLOCK), F32),
+            pltpu.VMEM((modes, n), F32),
+            pltpu.SemaphoreType.DMA,
         ],
         compiler_params=pltpu.CompilerParams(vmem_limit_bytes=GRANT),
     )(part, rest, start_basis.T)

time: 58 us -> 57 us (0.983)
  starting transfers between devices: 20.2 us -> 19.3 us
    ppermute x8, starting transfers between devices: 20.2 us -> 19.3 us  [swap(): return lax.ppermute(value, AXES, moves)]
where the time goes in v2:
time: 57 us; the launch traced here: 56.2 us
  waiting for transfers between devices  25.2 us (44%)
  starting transfers between devices  19.3 us (34%)
  Pallas kernels  6.05 us (11%)
  matrix products  2.68 us (5%)
  between operations  1.58 us (3%)
  local copies, waits for them, and re-layouts  0.95 us (2%)
    ppermute x8, waiting for transfers between devices, swap(): return lax.ppermute(value, AXES, moves)  25.2 us
    ppermute x8, starting transfers between devices, swap(): return lax.ppermute(value, AXES, moves)  19.3 us
    pallas_call x1, Pallas kernels, per_device(): pl.pallas_call(finish_kernel, out_shape=(jax.ShapeDtypeStruct((modes, row...  5.85 us
    dot_general x1, matrix products, per_device(): lax.dot_general(masked, masked, (((0,), (0,)), ((), ())), preferred_eleme...  2.68 us
  transfers between devices with their start and end apart: 8, of which 7 were waited for; matrix products, arithmetic and copies ran while one was open for 0% of the time, Pallas kernels for 0%

profile of v2, /device:TPU:0, one launch (start us, length us, event | category | flops | bytes accessed | tf_op | source)
XLA Modules:
  0.0 56.2 jit_solution(1304540826432549694)
XLA Ops:
  1.3 0.1 pad.9.clone
  1.4 2.7 %fusion = f32[512,512]{1,0:T(8,128)S(1)} fusion(bf16[1,1024,512]{2,1,0:T(8,128)(2,1)} %param.3, pred[1024]{0:T(1024)(128)(4,1)S(1)} %iota_compare_fusion.2), kind=kOutput, calls=%fused_computation | convolution fusion | flops 537395200 | bytes 2098176 | tf_op jit(solution)/shard_map/dot_general | solution.py:345
  4.2 0.1 maximum_maximum_fusion
  4.3 3.1 %collective-permute-start = (f32[2,264,128]{2,1,0:T(8,128)S(1)}, f32[2,264,128]{2,1,0:T(8,128)S(1)}, u32[]{:S(2)}, u32[]{:S(2)}) collective-permute-start(f32[2,264,128]{2,1,0:T(8,128)S(1)} %fusion.6), channel_id=1, source_target_pairs={{0,2},{1,3},{2,0},{3,1},{4,6},{5,7},{6,4},{7,5},{8,10},{9,11},{10,... | collective-permute-start | bytes 811016 | tf_op jit(solution)/shard_map/ppermute | solution.py:299
  7.5 4.4 %collective-permute-done = f32[2,264,128]{2,1,0:T(8,128)S(1)} collective-permute-done((f32[2,264,128]{2,1,0:T(8,128)S(1)}, f32[2,264,128]{2,1,0:T(8,128)S(1)}, u32[]{:S(2)}, u32[]{:S(2)}) %collective-permute-start) | collective-permute-done | bytes 270368 | tf_op jit(solution)/shard_map/ppermute | solution.py:299
  12.0 3.1 %collective-permute-start.1 = (f32[1,264,128]{2,1,0:T(8,128)S(1)}, f32[1,264,128]{2,1,0:T(8,128)S(1)}, u32[]{:S(2)}, u32[]{:S(2)}) collective-permute-start(f32[1,264,128]{2,1,0:T(8,128)S(1)} %slice_select_fusion), channel_id=1, source_target_pairs={{0,4},{1,5},{2,6},{3,7},{4,0},{5,1},{6,2},{7,3},{8,12},{9,13},{10,... | collective-permute-start | bytes 405512 | tf_op jit(solution)/shard_map/ppermute | solution.py:299
  15.1 4.4 %collective-permute-done.1 = f32[1,264,128]{2,1,0:T(8,128)S(1)} collective-permute-done((f32[1,264,128]{2,1,0:T(8,128)S(1)}, f32[1,264,128]{2,1,0:T(8,128)S(1)}, u32[]{:S(2)}, u32[]{:S(2)}) %collective-permute-start.1) | collective-permute-done | bytes 135200 | tf_op jit(solution)/shard_map/ppermute | solution.py:299
  19.6 1.9 %collective-permute-start.2 = (f32[1,264,128]{2,1,0:T(8,128)S(1)}, f32[1,264,128]{2,1,0:T(8,128)S(1)}, u32[]{:S(2)}, u32[]{:S(2)}) collective-permute-start(f32[1,264,128]{2,1,0:T(8,128)S(1)} %select_add_fusion.1), channel_id=1, source_target_pairs={{0,1},{1,0},{2,3},{3,2},{4,5},{5,4},{6,7},{7,6},{8,9},{9,8},{10,11... | collective-permute-start | bytes 405512 | tf_op jit(solution)/shard_map/ppermute | solution.py:299
  21.4 3.2 %collective-permute-done.2 = f32[1,264,128]{2,1,0:T(8,128)S(1)} collective-permute-done((f32[1,264,128]{2,1,0:T(8,128)S(1)}, f32[1,264,128]{2,1,0:T(8,128)S(1)}, u32[]{:S(2)}, u32[]{:S(2)}) %collective-permute-start.2) | collective-permute-done | bytes 135200 | tf_op jit(solution)/shard_map/ppermute | solution.py:299
  24.6 1.9 %collective-permute-start.3 = (f32[1,264,128]{2,1,0:T(8,128)S(1)}, f32[1,264,128]{2,1,0:T(8,128)S(1)}, u32[]{:S(2)}, u32[]{:S(2)}) collective-permute-start(f32[1,264,128]{2,1,0:T(8,128)S(1)} %add.14), channel_id=1, source_target_pairs={{0,8},{1,9},{2,10},{3,11},{4,12},{5,13},{6,14},{7,15},{8,0},{9,1},... | collective-permute-start | bytes 405512 | tf_op jit(solution)/shard_map/ppermute | solution.py:299
  26.6 3.8 %collective-permute-done.3 = f32[1,264,128]{2,1,0:T(8,128)S(1)} collective-permute-done((f32[1,264,128]{2,1,0:T(8,128)S(1)}, f32[1,264,128]{2,1,0:T(8,128)S(1)}, u32[]{:S(2)}, u32[]{:S(2)}) %collective-permute-start.3) | collective-permute-done | bytes 135200 | tf_op jit(solution)/shard_map/ppermute | solution.py:299
  30.4 2.8 %collective-permute-start.4 = (f32[1,264,128]{2,1,0:T(8,128)S(1)}, f32[1,264,128]{2,1,0:T(8,128)S(1)}, u32[]{:S(2)}, u32[]{:S(2)}) collective-permute-start(f32[1,264,128]{2,1,0:T(8,128)S(1)} %add.15), channel_id=1, source_target_pairs={{0,4},{1,5},{2,6},{3,7},{4,0},{5,1},{6,2},{7,3},{8,12},{9,13},{10,... | collective-permute-start | bytes 405512 | tf_op jit(solution)/shard_map/ppermute | solution.py:299
  33.2 3.2 %collective-permute-done.4 = f32[1,264,128]{2,1,0:T(8,128)S(1)} collective-permute-done((f32[1,264,128]{2,1,0:T(8,128)S(1)}, f32[1,264,128]{2,1,0:T(8,128)S(1)}, u32[]{:S(2)}, u32[]{:S(2)}) %collective-permute-start.4) | collective-permute-done | bytes 135200 | tf_op jit(solution)/shard_map/ppermute | solution.py:299
  36.4 2.3 %collective-permute-start.5 = (f32[2,264,128]{2,1,0:T(8,128)S(1)}, f32[2,264,128]{2,1,0:T(8,128)S(1)}, u32[]{:S(2)}, u32[]{:S(2)}) collective-permute-start(f32[2,264,128]{2,1,0:T(8,128)S(1)} %pad_maximum_fusion.2.part_ref), channel_id=1, source_target_pairs={{0,2},{1,3},{2,0},{3,1},{4,6},{5,7},{6,4},{7,5},{8,10},{9,11},{10,... | collective-permute-start | bytes 811016 | tf_op jit(solution)/shard_map/ppermute | solution.py:299
  38.7 4.4 %collective-permute-done.5.rest_ref = f32[2,264,128]{2,1,0:T(8,128)S(1)} collective-permute-done((f32[2,264,128]{2,1,0:T(8,128)S(1)}, f32[2,264,128]{2,1,0:T(8,128)S(1)}, u32[]{:S(2)}, u32[]{:S(2)}) %collective-permute-start.5) | collective-permute-done | bytes 270368 | tf_op jit(solution)/shard_map/ppermute | solution.py:299
  43.2 0.0 copy-start
  43.3 0.8 %copy-done.1 = f32[512,64]{0,1:T(8,128)S(1)} copy-done((f32[512,64]{0,1:T(8,128)S(1)}, f32[512,64]{0,1:T(8,128)}, u32[]{:S(2)}) %copy-start.1) | copy-done | bytes 131096
  44.1 0.2 shard_map.50.y_ref
  44.3 4.1 %collective-permute-start.6 = (f32[4,264,128]{2,1,0:T(8,128)S(1)}, f32[4,264,128]{2,1,0:T(8,128)S(1)}, u32[]{:S(2)}, u32[]{:S(2)}) collective-permute-start(f32[4,264,128]{2,1,0:T(8,128)S(1)} %pad_maximum_fusion.mine_ref), channel_id=1, source_target_pairs={{0,16},{1,17},{2,18},{3,19},{4,20},{5,21},{6,22},{7,23},{8,24},{9,... | collective-permute-start | bytes 1622024 | tf_op jit(solution)/shard_map/ppermute | solution.py:299
  48.4 0.1 collective-permute-start.7
  48.5 1.7 %collective-permute-done.7.y_other_ref = f32[64,512]{1,0:T(8,128)S(1)} collective-permute-done((f32[64,512]{1,0:T(8,128)S(1)}, f32[64,512]{1,0:T(8,128)S(1)}, u32[]{:S(2)}, u32[]{:S(2)}) %collective-permute-start.7) | collective-permute-done | bytes 131104 | tf_op jit(solution)/shard_map/ppermute | solution.py:299
  50.2 0.0 collective-permute-done.6.other_ref
  50.2 0.0 copy-done
  50.2 5.9 %shard_map.51 = (f32[64,1024]{1,0:T(8,128)}, f32[1,64]{1,0:T(1,128)}) custom-call(s32[1,1]{1,0:T(1,128)} %copy.11.valid_ref, f32[4,264,128]{2,1,0:T(8,128)S(1)} %pad_maximum_fusion.mine_ref, f32[4,264,128]{2,1,0:T(8,128)S(1)} %collective-permute-done.6.other_ref, f32[64,512]{1,0:T(8,128)S(1)} %shard_map.50.y_ref, ...), custom_call_target="tpu_custom_call" | custom-call | tf_op jit(solution)/shard_map/pallas_call | solution.py:367
  (22 shorter events, 0.4 us)
Async XLA Ops:
  4.3 7.6 %collective-permute-start = (f32[2,264,128]{2,1,0:T(8,128)S(1)}, f32[2,264,128]{2,1,0:T(8,128)S(1)}, u32[]{:S(2)}, u32[]{:S(2)}) collective-permute-start(f32[2,264,128]{2,1,0:T(8,128)S(1)} %fusion.6), channel_id=1, source_target_pairs={{0,2},{1,3},{2,0},{3,1},{4,6},{5,7},{6,4},{7,5},{8,10},{9,11},{10,... | collective-permute-start | bytes 811016 | tf_op jit(solution)/shard_map/ppermute | solution.py:299
  12.0 7.5 %collective-permute-start.1 = (f32[1,264,128]{2,1,0:T(8,128)S(1)}, f32[1,264,128]{2,1,0:T(8,128)S(1)}, u32[]{:S(2)}, u32[]{:S(2)}) collective-permute-start(f32[1,264,128]{2,1,0:T(8,128)S(1)} %slice_select_fusion), channel_id=1, source_target_pairs={{0,4},{1,5},{2,6},{3,7},{4,0},{5,1},{6,2},{7,3},{8,12},{9,13},{10,... | collective-permute-start | bytes 405512 | tf_op jit(solution)/shard_map/ppermute | solution.py:299
  19.6 5.1 %collective-permute-start.2 = (f32[1,264,128]{2,1,0:T(8,128)S(1)}, f32[1,264,128]{2,1,0:T(8,128)S(1)}, u32[]{:S(2)}, u32[]{:S(2)}) collective-permute-start(f32[1,264,128]{2,1,0:T(8,128)S(1)} %select_add_fusion.1), channel_id=1, source_target_pairs={{0,1},{1,0},{2,3},{3,2},{4,5},{5,4},{6,7},{7,6},{8,9},{9,8},{10,11... | collective-permute-start | bytes 405512 | tf_op jit(solution)/shard_map/ppermute | solution.py:299
  24.6 5.7 %collective-permute-start.3 = (f32[1,264,128]{2,1,0:T(8,128)S(1)}, f32[1,264,128]{2,1,0:T(8,128)S(1)}, u32[]{:S(2)}, u32[]{:S(2)}) collective-permute-start(f32[1,264,128]{2,1,0:T(8,128)S(1)} %add.14), channel_id=1, source_target_pairs={{0,8},{1,9},{2,10},{3,11},{4,12},{5,13},{6,14},{7,15},{8,0},{9,1},... | collective-permute-start | bytes 405512 | tf_op jit(solution)/shard_map/ppermute | solution.py:299
  30.4 6.0 %collective-permute-start.4 = (f32[1,264,128]{2,1,0:T(8,128)S(1)}, f32[1,264,128]{2,1,0:T(8,128)S(1)}, u32[]{:S(2)}, u32[]{:S(2)}) collective-permute-start(f32[1,264,128]{2,1,0:T(8,128)S(1)} %add.15), channel_id=1, source_target_pairs={{0,4},{1,5},{2,6},{3,7},{4,0},{5,1},{6,2},{7,3},{8,12},{9,13},{10,... | collective-permute-start | bytes 405512 | tf_op jit(solution)/shard_map/ppermute | solution.py:299
  36.4 6.7 %collective-permute-start.5 = (f32[2,264,128]{2,1,0:T(8,128)S(1)}, f32[2,264,128]{2,1,0:T(8,128)S(1)}, u32[]{:S(2)}, u32[]{:S(2)}) collective-permute-start(f32[2,264,128]{2,1,0:T(8,128)S(1)} %pad_maximum_fusion.2.part_ref), channel_id=1, source_target_pairs={{0,2},{1,3},{2,0},{3,1},{4,6},{5,7},{6,4},{7,5},{8,10},{9,11},{10,... | collective-permute-start | bytes 811016 | tf_op jit(solution)/shard_map/ppermute | solution.py:299
  43.2 0.9 %copy-start.1 = (f32[512,64]{0,1:T(8,128)S(1)}, f32[512,64]{0,1:T(8,128)}, u32[]{:S(2)}) copy-start(f32[512,64]{0,1:T(8,128)} %param.5) | copy-start | bytes 393220
  43.2 7.0 %copy-start = (bf16[1,1024,512]{2,1,0:T(8,128)(2,1)S(1)}, bf16[1,1024,512]{2,1,0:T(8,128)(2,1)}, u32[]{:S(2)}) copy-start(bf16[1,1024,512]{2,1,0:T(8,128)(2,1)} %param.3) | copy-start | bytes 3145732
  44.3 5.9 %collective-permute-start.6 = (f32[4,264,128]{2,1,0:T(8,128)S(1)}, f32[4,264,128]{2,1,0:T(8,128)S(1)}, u32[]{:S(2)}, u32[]{:S(2)}) collective-permute-start(f32[4,264,128]{2,1,0:T(8,128)S(1)} %pad_maximum_fusion.mine_ref), channel_id=1, source_target_pairs={{0,16},{1,17},{2,18},{3,19},{4,20},{5,21},{6,22},{7,23},{8,24},{9,... | collective-permute-start | bytes 1622024 | tf_op jit(solution)/shard_map/ppermute | solution.py:299
  48.4 1.7 %collective-permute-start.7 = (f32[64,512]{1,0:T(8,128)S(1)}, f32[64,512]{1,0:T(8,128)S(1)}, u32[]{:S(2)}, u32[]{:S(2)}) collective-permute-start(f32[64,512]{1,0:T(8,128)S(1)} %shard_map.50.y_ref), channel_id=1, source_target_pairs={{0,16},{1,17},{2,18},{3,19},{4,20},{5,21},{6,22},{7,23},{8,24},{9,... | collective-permute-start | bytes 393224 | tf_op jit(solution)/shard_map/ppermute | solution.py:299

commit v3 on v2

--- a/solution.py
+++ b/solution.py
@@ -28,15 +28,30 @@
     return high, middle, (rest - middle.astype(F32)).astype(jnp.bfloat16)
 
 
-def stacked(a, b, dim=0):
-    ah, am, al = thirds(a)
-    bh, bm, bl = thirds(b)
-    return lax.dot_general(
-        jnp.concatenate([ah, ah, am, ah, al, am], axis=dim),
-        jnp.concatenate([bh, bm, bh, bl, bh, bm], axis=0),
-        (((dim,), (0,)), ((), ())),
-        preferred_element_type=F32,
-    )
+def plain(a, b, ca=1, cb=0):
+    return lax.dot_general(a, b, (((ca,), (cb,)), ((), ())), preferred_element_type=F32)
+
+
+def left(parts, dim):
+    high, middle, low = parts
+    return jnp.concatenate([high, high, middle, high, low, middle], axis=dim)
+
+
+def right(parts):
+    high, middle, low = parts
+    return jnp.concatenate([high, middle, high, low, high, middle], axis=0)
+
+
+def stacked(a, b):
+    return plain(left(thirds(a), 0), right(thirds(b)), 0, 0)
+
+
+def two_thirds(a, b):
+    ah, am, _ = thirds(a)
+    bh, bm, _ = thirds(b)
+    rows = a.shape[0]
+    both = plain(jnp.concatenate([ah, am], axis=0), bh)
+    return both[:rows] + (both[rows:] + plain(ah, bm))
 
 
 def lane_copy(tile, lane):
@@ -176,28 +191,24 @@
     return slice(i * BLOCK, (i + 1) * BLOCK)
 
 
-def factor_kernel(part_ref, rest_ref, x_hbm, y_ref, s_ref, u_ref, x_ref, sem):
+def factor_kernel(mine_ref, x_hbm, y_ref, s_ref, x_ref, sem):
     @pl.when(lax.axis_index("field") == 0)
     def _():
         y_ref[...] = jnp.zeros_like(y_ref)
 
     @pl.when(lax.axis_index("field") == 1)
     def _():
-        apply_factor(part_ref, rest_ref, x_hbm, y_ref, s_ref, u_ref, x_ref, sem)
-
-
-def apply_factor(part_ref, rest_ref, x_hbm, y_ref, s_ref, u_ref, x_ref, sem):
+        apply_factor(mine_ref, x_hbm, y_ref, s_ref, x_ref, sem)
+
+
+def apply_factor(mine_ref, x_hbm, y_ref, s_ref, x_ref, sem):
     copy = pltpu.make_async_copy(x_hbm, x_ref, sem)
     copy.start()
     n = x_ref.shape[1]
     nb = n // BLOCK
-    half = part_ref.shape[0]
-    high = has_bit(bit_orders()[0])
 
     def read(part, start, rows):
-        a = part_ref[part % half, start : start + rows, :]
-        b = rest_ref[part % half, start : start + rows, :]
-        return jnp.where(high, a, b) if part >= half else jnp.where(high, b, a)
+        return mine_ref[part, start : start + rows, :]
 
     def put(i, j, v):
         s_ref[span(i), span(j)] = v
@@ -206,21 +217,35 @@
     for b in range(nb):
         lo, hi = b * BLOCK, (b + 1) * BLOCK
         tiles = [s_ref[lo + r : lo + r + TILE, lo:hi] for r in range(0, BLOCK, TILE)]
-        inverse = jnp.concatenate(inverse_factor(tiles, HALF), axis=0)
-        if hi < n:
-            near = stacked(inverse, s_ref[lo:hi, hi : hi + BLOCK], 1)
-            u_ref[:, hi : hi + BLOCK] = near
-            s_ref[span(b + 1), hi : hi + BLOCK] -= stacked(near, near)
+        inverse = left(thirds(jnp.concatenate(inverse_factor(tiles, HALF), axis=0)), 1)
+
+        def upper(columns):
+            return thirds(plain(inverse, right(thirds(s_ref[lo:hi, columns]))))
+
+        panels = []
+        for start, stop in ((hi, hi + BLOCK), (hi + BLOCK, n)):
+            if start < n:
+                panels.append((start, upper(slice(start, stop))))
+                if start == hi:
+                    near = left(panels[0][1], 0)
+                s_ref[span(b + 1), start:stop] -= plain(near, right(panels[-1][1]), 0, 0)
         if hi + BLOCK < n:
-            u_ref[:, hi + BLOCK :] = stacked(inverse, s_ref[lo:hi, hi + BLOCK :], 1)
-            s_ref[span(b + 1), hi + BLOCK :] -= stacked(near, u_ref[:, hi + BLOCK :])
-        u_ref[:, lo:hi] = stacked(inverse, s_ref[lo:hi, lo:hi], 1)
-        for i in range(b + 2, nb):
-            s_ref[span(i), i * BLOCK :] -= stacked(u_ref[:, span(i)], u_ref[:, i * BLOCK :])
+            far = panels[1][1]
+            for r in range(0, n - hi - BLOCK, BLOCK):
+                rows = slice(hi + BLOCK + r, hi + 2 * BLOCK + r)
+                s_ref[rows, rows.start :] -= plain(
+                    left([p[:, r : r + BLOCK] for p in far], 0),
+                    right([p[:, r:] for p in far]), 0, 0,
+                )
+        panels.append((lo, upper(slice(lo, hi))))
         if b == 0:
             copy.wait()
-        product = dot(x_ref[:, lo:hi], u_ref[:, lo:])
-        y_ref[:, lo:] = product if b == 0 else y_ref[:, lo:] + product
+        xh, xm, _ = thirds(x_ref[:, lo:hi])
+        x = jnp.concatenate([xh, xm, xh], axis=1)
+        for start, (uh, um, _) in panels:
+            product = plain(x, jnp.concatenate([uh, uh, um], axis=0))
+            columns = slice(start, start + uh.shape[1])
+            y_ref[:, columns] = product if b == 0 else y_ref[:, columns] + product
 
 
 def finish_kernel(
@@ -252,13 +277,13 @@
         return jnp.concatenate(inverse_factor(tiles, modes), axis=0)[:, :modes]
 
     y = jnp.where(first, y_other_ref[...], y_ref[...])
-    t = dot(y, g_ref[0])
+    t = two_thirds(y, g_ref[0])
     inverse = normal(dot(y, t, 1, 1))
-    q0 = dot(inverse, y)
-    z = dot(inverse, t)
-    w = dot(z, g_ref[1])
+    q0 = two_thirds(inverse, y)
+    z = two_thirds(inverse, t)
+    w = two_thirds(z, g_ref[1])
     inverse = normal(dot(z, w, 1, 1))
-    q1 = dot(inverse, z)
+    q1 = two_thirds(inverse, z)
     row, lane = iotas((modes, modes))
     diagonal = jnp.sum(jnp.where(row == lane, inverse, 0.0), axis=0, keepdims=True)
     strengths_ref[...] = 1.0 / diagonal
@@ -287,11 +312,11 @@
     sizes = [lax.axis_size(a) for a in AXES]
     moves = []
     for f in range(sizes[0]):
-        axis, b = which(f)
         for g in range(sizes[1]):
             for r in range(sizes[2]):
                 there = dict(zip(AXES, (f, g, r)))
-                there[axis] ^= 1 << b
+                for axis, b in which(f):
+                    there[axis] ^= 1 << b
                 here = (f * sizes[1] + g) * sizes[2] + r
                 moves.append(
                     (here, (there["field"] * sizes[1] + there["group"]) * sizes[2] + there["row"])
@@ -302,37 +327,41 @@
 def has_bit(which):
     def of(f):
         axis, b = which(f)
-        return (lax.axis_index(axis) >> b) & 1 == 1
+        return (lax.axis_index(axis) >> b) & 1
 
     return jnp.where(lax.axis_index("field") == 0, of(0), of(1))
 
 
-def bit_orders():
+def sum_all(value):
     sizes = {axis: lax.axis_size(axis) for axis in ("row", "group")}
+    if any(n & (n - 1) for n in sizes.values()) or min(sizes.values()) < 2:
+        return lax.psum(value, ("group", "row"))
     bits = {axis: n.bit_length() - 1 for axis, n in sizes.items()}
     order = [("row", 0), ("group", 0)]
     order += [(axis, b) for axis in ("row", "group") for b in range(1, bits[axis])]
-    return [lambda f, k=k: order[(k + 2 * (1 - f)) % len(order)] for k in range(len(order))]
-
-
-def joined(high, value, other):
-    return jnp.concatenate(
-        [jnp.where(high, other, value), jnp.where(high, value, other)], axis=0
-    )
-
-
-def sum_all(value):
-    orders = bit_orders()
-    for which in orders[:2]:
-        half = value.shape[0] // 2
-        high = has_bit(which)
-        keep = jnp.where(high, value[half:], value[:half])
-        send = jnp.where(high, value[:half], value[half:])
-        value = keep + swap(send, which)
-    for which in orders[2:]:
-        value = value + swap(value, which)
-    value = joined(has_bit(orders[1]), value, swap(value, orders[1]))
-    return value, swap(value, orders[0])
+    steps = [lambda f, k=k: order[(k + 2 * (1 - f)) % len(order)] for k in range(len(order))]
+    me = has_bit(steps[0]) + 2 * has_bit(steps[1])
+
+    def turned(d):
+        return lambda f: [steps[k](f) for k in range(2) if d >> k & 1]
+
+    others = (3, 1, 2)
+    arrived = [
+        swap(lax.dynamic_slice_in_dim(value, me ^ d, 1, 0), turned(d)) for d in others
+    ]
+    part = lax.dynamic_slice_in_dim(value, me, 1, 0)
+    for piece in arrived:
+        part = part + piece
+    for step in steps[2:]:
+        part = part + swap(part, lambda f, step=step: [step(f)])
+    held = {0: part} | {d: swap(part, turned(d)) for d in others}
+    parts = []
+    for q in range(4):
+        chosen = held[q]
+        for p in range(1, 4):
+            chosen = jnp.where(me == p, held[q ^ p], chosen)
+        parts.append(chosen)
+    return jnp.concatenate(parts, axis=0)
 
 
 def per_device(anomalies, valid_rows, start_basis):
@@ -345,23 +374,21 @@
     gram = lax.dot_general(
         masked, masked, (((0,), (0,)), ((), ())), preferred_element_type=F32
     )
-    part, rest = sum_all(pack(gram, ocean.astype(F32)))
-    mine = joined(has_bit(bit_orders()[0]), part, rest)
+    mine = sum_all(pack(gram, ocean.astype(F32)))
     y = pl.pallas_call(
         factor_kernel,
         out_shape=jax.ShapeDtypeStruct((modes, n), F32),
-        in_specs=[VMEM, VMEM, pl.BlockSpec(memory_space=pltpu.HBM)],
+        in_specs=[VMEM, pl.BlockSpec(memory_space=pltpu.HBM)],
         out_specs=VMEM,
         scratch_shapes=[
             pltpu.VMEM((n, n), F32),
-            pltpu.VMEM((BLOCK, n), F32),
             pltpu.VMEM((modes, n), F32),
             pltpu.SemaphoreType.DMA,
         ],
         compiler_params=pltpu.CompilerParams(vmem_limit_bytes=GRANT),
-    )(part, rest, start_basis.T)
+    )(mine, start_basis.T)
     y, mine = lax.optimization_barrier((y, mine))
-    partner = lambda f: ("field", 0)
+    partner = lambda f: [("field", 0)]
     y_other = swap(y, partner)
     other = swap(mine, partner)
     patterns, strengths = pl.pallas_call(

time: 57 us -> 50.8 us (0.89); the launches traced: 56.2 us -> 50.6 us
  waiting for transfers between devices: 25.2 us -> 22.3 us
  starting transfers between devices: 19.3 us -> 17.5 us
  Pallas kernels: 6.05 us -> 5.38 us
    ppermute x8 -> x10, waiting for transfers between devices: 25.2 us -> 22.3 us  [swap(): return lax.ppermute(value, AXES, moves)]
    ppermute x8 -> x10, starting transfers between devices: 19.3 us -> 17.5 us  [swap(): return lax.ppermute(value, AXES, moves)]
    pallas_call x1, Pallas kernels: 5.85 us -> 5.18 us  [per_device(): pl.pallas_call(finish_kernel, out_shape=(jax.ShapeDtypeStruct((modes, row...]
  transfers between devices with their start and end apart: 8 -> 10, of which waited for: 7 -> 8; matrix products, arithmetic and copies ran while one was open for 0% -> 0% of each run, Pallas kernels for 0% -> 0%
where the time goes in v3:
time: 50.8 us; the launch traced here: 50.6 us
  waiting for transfers between devices  22.3 us (44%)
  starting transfers between devices  17.5 us (34%)
  Pallas kernels  5.38 us (11%)
  matrix products  2.68 us (5%)
  between operations  1.57 us (3%)
  local copies, waits for them, and re-layouts  0.9 us (2%)
    ppermute x10, waiting for transfers between devices, swap(): return lax.ppermute(value, AXES, moves)  22.3 us
    ppermute x10, starting transfers between devices, swap(): return lax.ppermute(value, AXES, moves)  17.5 us
    pallas_call x1, Pallas kernels, per_device(): pl.pallas_call(finish_kernel, out_shape=(jax.ShapeDtypeStruct((modes, row...  5.18 us
    dot_general x1, matrix products, per_device(): lax.dot_general(masked, masked, (((0,), (0,)), ((), ())), preferred_eleme...  2.68 us
  transfers between devices with their start and end apart: 10, of which 8 were waited for; matrix products, arithmetic and copies ran while one was open for 0% of the time, Pallas kernels for 0%

profile of v3, /device:TPU:0, one launch (start us, length us, event | category | flops | bytes accessed | tf_op | source)
XLA Modules:
  0.0 50.6 jit_solution(3721745423715640248)
XLA Ops:
  1.3 2.7 %fusion = f32[512,512]{1,0:T(8,128)S(1)} fusion(bf16[1,1024,512]{2,1,0:T(8,128)(2,1)} %param.3, pred[1024]{0:T(1024)(128)(4,1)S(1)} %iota_compare_fusion.2), kind=kOutput, calls=%fused_computation.4 | convolution fusion | flops 537395200 | bytes 2098176 | tf_op jit(solution)/shard_map/dot_general | solution.py:374
  4.2 0.1 pad.9.clone
  4.2 0.1 maximum_maximum_fusion
  4.4 4.1 %collective-permute-start.2 = (f32[1,264,128]{2,1,0:T(8,128)S(1)}, f32[1,264,128]{2,1,0:T(8,128)S(1)}, u32[]{:S(2)}, u32[]{:S(2)}) collective-permute-start(f32[1,264,128]{2,1,0:T(8,128)S(1)} %get-tuple-element.19), channel_id=1, source_target_pairs={{0,4},{1,5},{2,6},{3,7},{4,0},{5,1},{6,2},{7,3},{8,12},{9,13},{10,... | collective-permute-start | bytes 405512 | tf_op jit(solution)/shard_map/ppermute | solution.py:324
  8.5 1.6 %collective-permute-start.1 = (f32[1,264,128]{2,1,0:T(8,128)S(1)}, f32[1,264,128]{2,1,0:T(8,128)S(1)}, u32[]{:S(2)}, u32[]{:S(2)}) collective-permute-start(f32[1,264,128]{2,1,0:T(8,128)S(1)} %get-tuple-element.18), channel_id=1, source_target_pairs={{0,2},{1,3},{2,0},{3,1},{4,6},{5,7},{6,4},{7,5},{8,10},{9,11},{10,... | collective-permute-start | bytes 405512 | tf_op jit(solution)/shard_map/ppermute | solution.py:324
  10.1 1.4 %collective-permute-done.2 = f32[1,264,128]{2,1,0:T(8,128)S(1)} collective-permute-done((f32[1,264,128]{2,1,0:T(8,128)S(1)}, f32[1,264,128]{2,1,0:T(8,128)S(1)}, u32[]{:S(2)}, u32[]{:S(2)}) %collective-permute-start.2) | collective-permute-done | bytes 135200 | tf_op jit(solution)/shard_map/ppermute | solution.py:324
  11.5 2.0 %collective-permute-done.1 = f32[1,264,128]{2,1,0:T(8,128)S(1)} collective-permute-done((f32[1,264,128]{2,1,0:T(8,128)S(1)}, f32[1,264,128]{2,1,0:T(8,128)S(1)}, u32[]{:S(2)}, u32[]{:S(2)}) %collective-permute-start.1) | collective-permute-done | bytes 135200 | tf_op jit(solution)/shard_map/ppermute | solution.py:324
  13.5 3.5 %collective-permute-done = f32[1,264,128]{2,1,0:T(8,128)S(1)} collective-permute-done((f32[1,264,128]{2,1,0:T(8,128)S(1)}, f32[1,264,128]{2,1,0:T(8,128)S(1)}, u32[]{:S(2)}, u32[]{:S(2)}) %collective-permute-start) | collective-permute-done | bytes 135200 | tf_op jit(solution)/shard_map/ppermute | solution.py:324
  17.0 1.6 %collective-permute-start.3 = (f32[1,264,128]{2,1,0:T(8,128)S(1)}, f32[1,264,128]{2,1,0:T(8,128)S(1)}, u32[]{:S(2)}, u32[]{:S(2)}) collective-permute-start(f32[1,264,128]{2,1,0:T(8,128)S(1)} %fusion.9), channel_id=1, source_target_pairs={{0,1},{1,0},{2,3},{3,2},{4,5},{5,4},{6,7},{7,6},{8,9},{9,8},{10,11... | collective-permute-start | bytes 405512 | tf_op jit(solution)/shard_map/ppermute | solution.py:324
  18.6 3.5 %collective-permute-done.3 = f32[1,264,128]{2,1,0:T(8,128)S(1)} collective-permute-done((f32[1,264,128]{2,1,0:T(8,128)S(1)}, f32[1,264,128]{2,1,0:T(8,128)S(1)}, u32[]{:S(2)}, u32[]{:S(2)}) %collective-permute-start.3) | collective-permute-done | bytes 135200 | tf_op jit(solution)/shard_map/ppermute | solution.py:324
  22.1 1.6 %collective-permute-start.4 = (f32[1,264,128]{2,1,0:T(8,128)S(1)}, f32[1,264,128]{2,1,0:T(8,128)S(1)}, u32[]{:S(2)}, u32[]{:S(2)}) collective-permute-start(f32[1,264,128]{2,1,0:T(8,128)S(1)} %add.38), channel_id=1, source_target_pairs={{0,8},{1,9},{2,10},{3,11},{4,12},{5,13},{6,14},{7,15},{8,0},{9,1},... | collective-permute-start | bytes 405512 | tf_op jit(solution)/shard_map/ppermute | solution.py:324
  23.7 3.5 %collective-permute-done.4 = f32[1,264,128]{2,1,0:T(8,128)S(1)} collective-permute-done((f32[1,264,128]{2,1,0:T(8,128)S(1)}, f32[1,264,128]{2,1,0:T(8,128)S(1)}, u32[]{:S(2)}, u32[]{:S(2)}) %collective-permute-start.4) | collective-permute-done | bytes 135200 | tf_op jit(solution)/shard_map/ppermute | solution.py:324
  27.2 1.5 %collective-permute-start.5 = (f32[1,264,128]{2,1,0:T(8,128)S(1)}, f32[1,264,128]{2,1,0:T(8,128)S(1)}, u32[]{:S(2)}, u32[]{:S(2)}) collective-permute-start(f32[1,264,128]{2,1,0:T(8,128)S(1)} %add.39), channel_id=1, source_target_pairs={{0,6},{1,7},{2,4},{3,5},{4,2},{5,3},{6,0},{7,1},{8,14},{9,15},{10,... | collective-permute-start | bytes 405512 | tf_op jit(solution)/shard_map/ppermute | solution.py:324
  28.7 2.5 %collective-permute-start.6 = (f32[1,264,128]{2,1,0:T(8,128)S(1)}, f32[1,264,128]{2,1,0:T(8,128)S(1)}, u32[]{:S(2)}, u32[]{:S(2)}) collective-permute-start(f32[1,264,128]{2,1,0:T(8,128)S(1)} %add.39), channel_id=1, source_target_pairs={{0,4},{1,5},{2,6},{3,7},{4,0},{5,1},{6,2},{7,3},{8,12},{9,13},{10,... | collective-permute-start | bytes 405512 | tf_op jit(solution)/shard_map/ppermute | solution.py:324
  31.3 0.5 collective-permute-start.7
  31.8 2.4 %collective-permute-done.5 = f32[1,264,128]{2,1,0:T(8,128)S(1)} collective-permute-done((f32[1,264,128]{2,1,0:T(8,128)S(1)}, f32[1,264,128]{2,1,0:T(8,128)S(1)}, u32[]{:S(2)}, u32[]{:S(2)}) %collective-permute-start.5) | collective-permute-done | bytes 135200 | tf_op jit(solution)/shard_map/ppermute | solution.py:324
  34.2 4.2 %collective-permute-done.6 = f32[1,264,128]{2,1,0:T(8,128)S(1)} collective-permute-done((f32[1,264,128]{2,1,0:T(8,128)S(1)}, f32[1,264,128]{2,1,0:T(8,128)S(1)}, u32[]{:S(2)}, u32[]{:S(2)}) %collective-permute-start.6) | collective-permute-done | bytes 135200 | tf_op jit(solution)/shard_map/ppermute | solution.py:324
  38.4 0.1 select_select_fusion.3
  38.6 0.8 %copy-done.1 = f32[512,64]{0,1:T(8,128)S(1)} copy-done((f32[512,64]{0,1:T(8,128)S(1)}, f32[512,64]{0,1:T(8,128)}, u32[]{:S(2)}) %copy-start.1) | copy-done | bytes 131096
  39.3 0.2 shard_map.50.y_ref
  39.5 4.0 %collective-permute-start.8 = (f32[4,264,128]{2,1,0:T(8,128)S(1)}, f32[4,264,128]{2,1,0:T(8,128)S(1)}, u32[]{:S(2)}, u32[]{:S(2)}) collective-permute-start(f32[4,264,128]{2,1,0:T(8,128)S(1)} %pad_maximum_fusion.mine_ref), channel_id=1, source_target_pairs={{0,16},{1,17},{2,18},{3,19},{4,20},{5,21},{6,22},{7,23},{8,24},{9,... | collective-permute-start | bytes 1622024 | tf_op jit(solution)/shard_map/ppermute | solution.py:324
  43.5 0.1 collective-permute-start.9
  43.6 1.7 %collective-permute-done.9.y_other_ref = f32[64,512]{1,0:T(8,128)S(1)} collective-permute-done((f32[64,512]{1,0:T(8,128)S(1)}, f32[64,512]{1,0:T(8,128)S(1)}, u32[]{:S(2)}, u32[]{:S(2)}) %collective-permute-start.9) | collective-permute-done | bytes 131104 | tf_op jit(solution)/shard_map/ppermute | solution.py:324
  45.3 5.2 %shard_map.51 = (f32[64,1024]{1,0:T(8,128)}, f32[1,64]{1,0:T(1,128)}) custom-call(s32[1,1]{1,0:T(1,128)} %copy.11.valid_ref, f32[4,264,128]{2,1,0:T(8,128)S(1)} %pad_maximum_fusion.mine_ref, f32[4,264,128]{2,1,0:T(8,128)S(1)} %collective-permute-done.8.other_ref, f32[64,512]{1,0:T(8,128)S(1)} %shard_map.50.y_ref, ...), custom_call_target="tpu_custom_call" | custom-call | tf_op jit(solution)/shard_map/pallas_call | solution.py:394
  (22 shorter events, 0.3 us)
Async XLA Ops:
  4.4 7.1 %collective-permute-start.2 = (f32[1,264,128]{2,1,0:T(8,128)S(1)}, f32[1,264,128]{2,1,0:T(8,128)S(1)}, u32[]{:S(2)}, u32[]{:S(2)}) collective-permute-start(f32[1,264,128]{2,1,0:T(8,128)S(1)} %get-tuple-element.19), channel_id=1, source_target_pairs={{0,4},{1,5},{2,6},{3,7},{4,0},{5,1},{6,2},{7,3},{8,12},{9,13},{10,... | collective-permute-start | bytes 405512 | tf_op jit(solution)/shard_map/ppermute | solution.py:324
  8.5 5.0 %collective-permute-start.1 = (f32[1,264,128]{2,1,0:T(8,128)S(1)}, f32[1,264,128]{2,1,0:T(8,128)S(1)}, u32[]{:S(2)}, u32[]{:S(2)}) collective-permute-start(f32[1,264,128]{2,1,0:T(8,128)S(1)} %get-tuple-element.18), channel_id=1, source_target_pairs={{0,2},{1,3},{2,0},{3,1},{4,6},{5,7},{6,4},{7,5},{8,10},{9,11},{10,... | collective-permute-start | bytes 405512 | tf_op jit(solution)/shard_map/ppermute | solution.py:324
  10.1 6.9 %collective-permute-start = (f32[1,264,128]{2,1,0:T(8,128)S(1)}, f32[1,264,128]{2,1,0:T(8,128)S(1)}, u32[]{:S(2)}, u32[]{:S(2)}) collective-permute-start(f32[1,264,128]{2,1,0:T(8,128)S(1)} %get-tuple-element.17), channel_id=1, source_target_pairs={{0,6},{1,7},{2,4},{3,5},{4,2},{5,3},{6,0},{7,1},{8,14},{9,15},{10,... | collective-permute-start | bytes 405512 | tf_op jit(solution)/shard_map/ppermute | solution.py:324
  17.0 5.1 %collective-permute-start.3 = (f32[1,264,128]{2,1,0:T(8,128)S(1)}, f32[1,264,128]{2,1,0:T(8,128)S(1)}, u32[]{:S(2)}, u32[]{:S(2)}) collective-permute-start(f32[1,264,128]{2,1,0:T(8,128)S(1)} %fusion.9), channel_id=1, source_target_pairs={{0,1},{1,0},{2,3},{3,2},{4,5},{5,4},{6,7},{7,6},{8,9},{9,8},{10,11... | collective-permute-start | bytes 405512 | tf_op jit(solution)/shard_map/ppermute | solution.py:324
  22.1 5.1 %collective-permute-start.4 = (f32[1,264,128]{2,1,0:T(8,128)S(1)}, f32[1,264,128]{2,1,0:T(8,128)S(1)}, u32[]{:S(2)}, u32[]{:S(2)}) collective-permute-start(f32[1,264,128]{2,1,0:T(8,128)S(1)} %add.38), channel_id=1, source_target_pairs={{0,8},{1,9},{2,10},{3,11},{4,12},{5,13},{6,14},{7,15},{8,0},{9,1},... | collective-permute-start | bytes 405512 | tf_op jit(solution)/shard_map/ppermute | solution.py:324
  27.2 7.0 %collective-permute-start.5 = (f32[1,264,128]{2,1,0:T(8,128)S(1)}, f32[1,264,128]{2,1,0:T(8,128)S(1)}, u32[]{:S(2)}, u32[]{:S(2)}) collective-permute-start(f32[1,264,128]{2,1,0:T(8,128)S(1)} %add.39), channel_id=1, source_target_pairs={{0,6},{1,7},{2,4},{3,5},{4,2},{5,3},{6,0},{7,1},{8,14},{9,15},{10,... | collective-permute-start | bytes 405512 | tf_op jit(solution)/shard_map/ppermute | solution.py:324
  28.7 9.7 %collective-permute-start.6 = (f32[1,264,128]{2,1,0:T(8,128)S(1)}, f32[1,264,128]{2,1,0:T(8,128)S(1)}, u32[]{:S(2)}, u32[]{:S(2)}) collective-permute-start(f32[1,264,128]{2,1,0:T(8,128)S(1)} %add.39), channel_id=1, source_target_pairs={{0,4},{1,5},{2,6},{3,7},{4,0},{5,1},{6,2},{7,3},{8,12},{9,13},{10,... | collective-permute-start | bytes 405512 | tf_op jit(solution)/shard_map/ppermute | solution.py:324
  31.3 7.2 %collective-permute-start.7 = (f32[1,264,128]{2,1,0:T(8,128)S(1)}, f32[1,264,128]{2,1,0:T(8,128)S(1)}, u32[]{:S(2)}, u32[]{:S(2)}) collective-permute-start(f32[1,264,128]{2,1,0:T(8,128)S(1)} %add.39), channel_id=1, source_target_pairs={{0,2},{1,3},{2,0},{3,1},{4,6},{5,7},{6,4},{7,5},{8,10},{9,11},{10,... | collective-permute-start | bytes 405512 | tf_op jit(solution)/shard_map/ppermute | solution.py:324
  38.4 0.9 %copy-start.1 = (f32[512,64]{0,1:T(8,128)S(1)}, f32[512,64]{0,1:T(8,128)}, u32[]{:S(2)}) copy-start(f32[512,64]{0,1:T(8,128)} %param.5) | copy-start | bytes 393220
  38.5 6.8 %copy-start = (bf16[1,1024,512]{2,1,0:T(8,128)(2,1)S(1)}, bf16[1,1024,512]{2,1,0:T(8,128)(2,1)}, u32[]{:S(2)}) copy-start(bf16[1,1024,512]{2,1,0:T(8,128)(2,1)} %param.3) | copy-start | bytes 3145732
  39.5 5.7 %collective-permute-start.8 = (f32[4,264,128]{2,1,0:T(8,128)S(1)}, f32[4,264,128]{2,1,0:T(8,128)S(1)}, u32[]{:S(2)}, u32[]{:S(2)}) collective-permute-start(f32[4,264,128]{2,1,0:T(8,128)S(1)} %pad_maximum_fusion.mine_ref), channel_id=1, source_target_pairs={{0,16},{1,17},{2,18},{3,19},{4,20},{5,21},{6,22},{7,23},{8,24},{9,... | collective-permute-start | bytes 1622024 | tf_op jit(solution)/shard_map/ppermute | solution.py:324
  43.5 1.7 %collective-permute-start.9 = (f32[64,512]{1,0:T(8,128)S(1)}, f32[64,512]{1,0:T(8,128)S(1)}, u32[]{:S(2)}, u32[]{:S(2)}) collective-permute-start(f32[64,512]{1,0:T(8,128)S(1)} %shard_map.50.y_ref), channel_id=1, source_target_pairs={{0,16},{1,17},{2,18},{3,19},{4,20},{5,21},{6,22},{7,23},{8,24},{9,... | collective-permute-start | bytes 393224 | tf_op jit(solution)/shard_map/ppermute | solution.py:324

commit v4 on v3

--- a/solution.py
+++ b/solution.py
@@ -114,7 +114,7 @@
     return out
 
 
-def inverse_factor(tiles, size):
+def inverse_factor(tiles, size, between=lambda: None):
     tiles = list(tiles)
     out = []
     count = size // TILE
@@ -122,6 +122,8 @@
     for base in range(0, len(tiles) * TILE, size):
         done = eliminate(tiles[:count], base)
         out += done
+        if base == 0:
+            between()
         tiles = tiles[count:]
         if tiles:
             rows = jnp.concatenate(done, axis=0)
@@ -214,38 +216,44 @@
         s_ref[span(i), span(j)] = v
 
     unpack(read, nb, put)
+    later = lambda: None
     for b in range(nb):
         lo, hi = b * BLOCK, (b + 1) * BLOCK
+        far = hi + BLOCK
         tiles = [s_ref[lo + r : lo + r + TILE, lo:hi] for r in range(0, BLOCK, TILE)]
-        inverse = left(thirds(jnp.concatenate(inverse_factor(tiles, HALF), axis=0)), 1)
-
-        def upper(columns):
-            return thirds(plain(inverse, right(thirds(s_ref[lo:hi, columns]))))
-
-        panels = []
-        for start, stop in ((hi, hi + BLOCK), (hi + BLOCK, n)):
-            if start < n:
-                panels.append((start, upper(slice(start, stop))))
-                if start == hi:
-                    near = left(panels[0][1], 0)
-                s_ref[span(b + 1), start:stop] -= plain(near, right(panels[-1][1]), 0, 0)
-        if hi + BLOCK < n:
-            far = panels[1][1]
-            for r in range(0, n - hi - BLOCK, BLOCK):
-                rows = slice(hi + BLOCK + r, hi + 2 * BLOCK + r)
-                s_ref[rows, rows.start :] -= plain(
-                    left([p[:, r : r + BLOCK] for p in far], 0),
-                    right([p[:, r:] for p in far]), 0, 0,
-                )
-        panels.append((lo, upper(slice(lo, hi))))
-        if b == 0:
-            copy.wait()
-        xh, xm, _ = thirds(x_ref[:, lo:hi])
-        x = jnp.concatenate([xh, xm, xh], axis=1)
-        for start, (uh, um, _) in panels:
-            product = plain(x, jnp.concatenate([uh, uh, um], axis=0))
-            columns = slice(start, start + uh.shape[1])
-            y_ref[:, columns] = product if b == 0 else y_ref[:, columns] + product
+        inverse = jnp.concatenate(inverse_factor(tiles, HALF, later), axis=0)
+        inverse = left(thirds(inverse), 1)
+
+        def upper(start, stop, inverse=inverse, lo=lo, hi=hi):
+            return thirds(plain(inverse, right(thirds(s_ref[lo:hi, start:stop]))))
+
+        near = None
+        if hi < n:
+            near = upper(hi, far)
+            s_ref[span(b + 1), hi:far] -= plain(left(near, 0), right(near), 0, 0)
+
+        def later(b=b, lo=lo, hi=hi, far=far, near=near, upper=upper):
+            panels = [] if near is None else [(hi, near)]
+            if far < n:
+                rest = upper(far, n)
+                panels.append((far, rest))
+                s_ref[hi:far, far:] -= plain(left(near, 0), right(rest), 0, 0)
+                for r in range(0, n - far, BLOCK):
+                    s_ref[far + r : far + r + BLOCK, far + r :] -= plain(
+                        left([p[:, r : r + BLOCK] for p in rest], 0),
+                        right([p[:, r:] for p in rest]), 0, 0,
+                    )
+            panels.append((lo, upper(lo, hi)))
+            if b == 0:
+                copy.wait()
+            xh, xm, _ = thirds(x_ref[:, lo:hi])
+            x = jnp.concatenate([xh, xm, xh], axis=1)
+            for start, (uh, um, _) in panels:
+                product = plain(x, jnp.concatenate([uh, uh, um], axis=0))
+                columns = slice(start, start + uh.shape[1])
+                y_ref[:, columns] = product if b == 0 else y_ref[:, columns] + product
+
+    later()
 
 
 def finish_kernel(
@@ -257,14 +265,15 @@
     modes, n = y_ref.shape
     nb = n // BLOCK
     first = lax.axis_index("field") == 0
-    for f in range(2):
-
-        def read(part, start, rows, f=f):
+
+    def fill(f):
+
+        def read(part, start, rows):
             a = mine_ref[part, start : start + rows, :]
             b = other_ref[part, start : start + rows, :]
             return jnp.where(first, a, b) if f == 0 else jnp.where(first, b, a)
 
-        def put(i, j, v, f=f):
+        def put(i, j, v):
             g_ref[f, span(i), span(j)] = v
             if i != j:
                 g_ref[f, span(j), span(i)] = v.T
@@ -277,8 +286,11 @@
         return jnp.concatenate(inverse_factor(tiles, modes), axis=0)[:, :modes]
 
     y = jnp.where(first, y_other_ref[...], y_ref[...])
+    fill(0)
     t = two_thirds(y, g_ref[0])
-    inverse = normal(dot(y, t, 1, 1))
+    product = dot(y, t, 1, 1)
+    fill(1)
+    inverse = normal(product)
     q0 = two_thirds(inverse, y)
     z = two_thirds(inverse, t)
     w = two_thirds(z, g_ref[1])
@@ -342,8 +354,8 @@
     steps = [lambda f, k=k: order[(k + 2 * (1 - f)) % len(order)] for k in range(len(order))]
     me = has_bit(steps[0]) + 2 * has_bit(steps[1])
 
-    def turned(d):
-        return lambda f: [steps[k](f) for k in range(2) if d >> k & 1]
+    def turned(d, first=0):
+        return lambda f: [step(f) for k, step in enumerate(steps[first : first + 2]) if d >> k & 1]
 
     others = (3, 1, 2)
     arrived = [
@@ -352,8 +364,11 @@
     part = lax.dynamic_slice_in_dim(value, me, 1, 0)
     for piece in arrived:
         part = part + piece
-    for step in steps[2:]:
-        part = part + swap(part, lambda f, step=step: [step(f)])
+    for first in range(2, len(steps), 2):
+        ways = (1, 2, 3) if first + 1 < len(steps) else (1,)
+        arrived = [swap(part, turned(d, first)) for d in ways]
+        for piece in arrived:
+            part = part + piece
     held = {0: part} | {d: swap(part, turned(d)) for d in others}
     parts = []
     for q in range(4):
@@ -386,7 +401,7 @@
             pltpu.SemaphoreType.DMA,
         ],
         compiler_params=pltpu.CompilerParams(vmem_limit_bytes=GRANT),
-    )(mine, start_basis.T)
+    )(mine, pltpu.with_memory_space_constraint(start_basis.T, pltpu.HBM))
     y, mine = lax.optimization_barrier((y, mine))
     partner = lambda f: [("field", 0)]
     y_other = swap(y, partner)

time: 50.8 us -> 48.7 us (0.959)
  waiting for transfers between devices: 22.3 us -> 18.4 us
  starting transfers between devices: 17.5 us -> 20 us
  local copies, waits for them, and re-layouts: 0.9 us -> 0.14 us
    ppermute x10 -> x11, waiting for transfers between devices: 22.3 us -> 18.4 us  [swap(): return lax.ppermute(value, AXES, moves)]
    ppermute x10 -> x11, starting transfers between devices: 17.5 us -> 20 us  [swap(): return lax.ppermute(value, AXES, moves)]
    unnamed x7 -> x5, local copies, waits for them, and re-layouts: 0.8 us -> 0.04 us
  transfers between devices with their start and end apart: 10 -> 11, of which waited for: 8 -> 9; matrix products, arithmetic and copies ran while one was open for 0% -> 0% of each run, Pallas kernels for 0% -> 0%
where the time goes in v4:
time: 48.7 us; the launch traced here: 48.5 us
  starting transfers between devices  20 us (41%)
  waiting for transfers between devices  18.4 us (38%)
  Pallas kernels  5.39 us (11%)
  matrix products  2.68 us (6%)
  between operations  1.57 us (3%)
    ppermute x11, starting transfers between devices, swap(): return lax.ppermute(value, AXES, moves)  20 us
    ppermute x11, waiting for transfers between devices, swap(): return lax.ppermute(value, AXES, moves)  18.4 us
    pallas_call x1, Pallas kernels, per_device(): pl.pallas_call(finish_kernel, out_shape=(jax.ShapeDtypeStruct((modes, row...  5.18 us
    dot_general x1, matrix products, per_device(): lax.dot_general(masked, masked, (((0,), (0,)), ((), ())), preferred_eleme...  2.68 us
  transfers between devices with their start and end apart: 11, of which 9 were waited for; matrix products, arithmetic and copies ran while one was open for 0% of the time, Pallas kernels for 0%

profile of v4, /device:TPU:0, one launch (start us, length us, event | category | flops | bytes accessed | tf_op | source)
XLA Modules:
  0.0 48.5 jit_solution(10964830958186347120)
XLA Ops:
  1.3 2.7 %fusion = f32[512,512]{1,0:T(8,128)S(1)} fusion(bf16[1,1024,512]{2,1,0:T(8,128)(2,1)} %param.3, pred[1024]{0:T(1024)(128)(4,1)S(1)} %iota_compare_fusion.2), kind=kOutput, calls=%fused_computation.4 | convolution fusion | flops 537395200 | bytes 2098176 | tf_op jit(solution)/shard_map/dot_general | solution.py:389
  4.2 0.1 pad.9.clone
  4.2 0.1 maximum_maximum_fusion
  4.4 4.1 %collective-permute-start.2 = (f32[1,264,128]{2,1,0:T(8,128)S(1)}, f32[1,264,128]{2,1,0:T(8,128)S(1)}, u32[]{:S(2)}, u32[]{:S(2)}) collective-permute-start(f32[1,264,128]{2,1,0:T(8,128)S(1)} %get-tuple-element.19), channel_id=1, source_target_pairs={{0,4},{1,5},{2,6},{3,7},{4,0},{5,1},{6,2},{7,3},{8,12},{9,13},{10,... | collective-permute-start | bytes 405512 | tf_op jit(solution)/shard_map/ppermute | solution.py:336
  8.5 1.6 %collective-permute-start.1 = (f32[1,264,128]{2,1,0:T(8,128)S(1)}, f32[1,264,128]{2,1,0:T(8,128)S(1)}, u32[]{:S(2)}, u32[]{:S(2)}) collective-permute-start(f32[1,264,128]{2,1,0:T(8,128)S(1)} %get-tuple-element.18), channel_id=1, source_target_pairs={{0,2},{1,3},{2,0},{3,1},{4,6},{5,7},{6,4},{7,5},{8,10},{9,11},{10,... | collective-permute-start | bytes 405512 | tf_op jit(solution)/shard_map/ppermute | solution.py:336
  10.1 1.4 %collective-permute-done.2 = f32[1,264,128]{2,1,0:T(8,128)S(1)} collective-permute-done((f32[1,264,128]{2,1,0:T(8,128)S(1)}, f32[1,264,128]{2,1,0:T(8,128)S(1)}, u32[]{:S(2)}, u32[]{:S(2)}) %collective-permute-start.2) | collective-permute-done | bytes 135200 | tf_op jit(solution)/shard_map/ppermute | solution.py:336
  11.5 2.0 %collective-permute-done.1 = f32[1,264,128]{2,1,0:T(8,128)S(1)} collective-permute-done((f32[1,264,128]{2,1,0:T(8,128)S(1)}, f32[1,264,128]{2,1,0:T(8,128)S(1)}, u32[]{:S(2)}, u32[]{:S(2)}) %collective-permute-start.1) | collective-permute-done | bytes 135200 | tf_op jit(solution)/shard_map/ppermute | solution.py:336
  13.5 3.4 %collective-permute-done = f32[1,264,128]{2,1,0:T(8,128)S(1)} collective-permute-done((f32[1,264,128]{2,1,0:T(8,128)S(1)}, f32[1,264,128]{2,1,0:T(8,128)S(1)}, u32[]{:S(2)}, u32[]{:S(2)}) %collective-permute-start) | collective-permute-done | bytes 135200 | tf_op jit(solution)/shard_map/ppermute | solution.py:336
  16.9 2.6 %collective-permute-start.5 = (f32[1,264,128]{2,1,0:T(8,128)S(1)}, f32[1,264,128]{2,1,0:T(8,128)S(1)}, u32[]{:S(2)}, u32[]{:S(2)}) collective-permute-start(f32[1,264,128]{2,1,0:T(8,128)S(1)} %fusion.9), channel_id=1, source_target_pairs={{0,9},{1,8},{2,11},{3,10},{4,13},{5,12},{6,15},{7,14},{8,1},{9,0},... | collective-permute-start | bytes 405512 | tf_op jit(solution)/shard_map/ppermute | solution.py:336
  19.5 0.5 %collective-permute-start.4 = (f32[1,264,128]{2,1,0:T(8,128)S(1)}, f32[1,264,128]{2,1,0:T(8,128)S(1)}, u32[]{:S(2)}, u32[]{:S(2)}) collective-permute-start(f32[1,264,128]{2,1,0:T(8,128)S(1)} %fusion.9), channel_id=1, source_target_pairs={{0,8},{1,9},{2,10},{3,11},{4,12},{5,13},{6,14},{7,15},{8,0},{9,1},... | collective-permute-start | bytes 405512 | tf_op jit(solution)/shard_map/ppermute | solution.py:336
  20.0 0.5 collective-permute-start.3
  20.5 2.4 %collective-permute-done.5 = f32[1,264,128]{2,1,0:T(8,128)S(1)} collective-permute-done((f32[1,264,128]{2,1,0:T(8,128)S(1)}, f32[1,264,128]{2,1,0:T(8,128)S(1)}, u32[]{:S(2)}, u32[]{:S(2)}) %collective-permute-start.5) | collective-permute-done | bytes 135200 | tf_op jit(solution)/shard_map/ppermute | solution.py:336
  22.9 1.6 %collective-permute-done.4 = f32[1,264,128]{2,1,0:T(8,128)S(1)} collective-permute-done((f32[1,264,128]{2,1,0:T(8,128)S(1)}, f32[1,264,128]{2,1,0:T(8,128)S(1)}, u32[]{:S(2)}, u32[]{:S(2)}) %collective-permute-start.4) | collective-permute-done | bytes 135200 | tf_op jit(solution)/shard_map/ppermute | solution.py:336
  24.5 0.5 %collective-permute-done.3 = f32[1,264,128]{2,1,0:T(8,128)S(1)} collective-permute-done((f32[1,264,128]{2,1,0:T(8,128)S(1)}, f32[1,264,128]{2,1,0:T(8,128)S(1)}, u32[]{:S(2)}, u32[]{:S(2)}) %collective-permute-start.3) | collective-permute-done | bytes 135200 | tf_op jit(solution)/shard_map/ppermute | solution.py:336
  25.1 1.5 %collective-permute-start.6 = (f32[1,264,128]{2,1,0:T(8,128)S(1)}, f32[1,264,128]{2,1,0:T(8,128)S(1)}, u32[]{:S(2)}, u32[]{:S(2)}) collective-permute-start(f32[1,264,128]{2,1,0:T(8,128)S(1)} %add_add_fusion), channel_id=1, source_target_pairs={{0,6},{1,7},{2,4},{3,5},{4,2},{5,3},{6,0},{7,1},{8,14},{9,15},{10,... | collective-permute-start | bytes 405512 | tf_op jit(solution)/shard_map/ppermute | solution.py:336
  26.6 6.2 %collective-permute-start.7 = (f32[1,264,128]{2,1,0:T(8,128)S(1)}, f32[1,264,128]{2,1,0:T(8,128)S(1)}, u32[]{:S(2)}, u32[]{:S(2)}) collective-permute-start(f32[1,264,128]{2,1,0:T(8,128)S(1)} %add_add_fusion), channel_id=1, source_target_pairs={{0,4},{1,5},{2,6},{3,7},{4,0},{5,1},{6,2},{7,3},{8,12},{9,13},{10,... | collective-permute-start | bytes 405512 | tf_op jit(solution)/shard_map/ppermute | solution.py:336
  32.8 0.5 %collective-permute-start.8 = (f32[1,264,128]{2,1,0:T(8,128)S(1)}, f32[1,264,128]{2,1,0:T(8,128)S(1)}, u32[]{:S(2)}, u32[]{:S(2)}) collective-permute-start(f32[1,264,128]{2,1,0:T(8,128)S(1)} %add_add_fusion), channel_id=1, source_target_pairs={{0,2},{1,3},{2,0},{3,1},{4,6},{5,7},{6,4},{7,5},{8,10},{9,11},{10,... | collective-permute-start | bytes 405512 | tf_op jit(solution)/shard_map/ppermute | solution.py:336
  33.3 4.0 %collective-permute-done.7 = f32[1,264,128]{2,1,0:T(8,128)S(1)} collective-permute-done((f32[1,264,128]{2,1,0:T(8,128)S(1)}, f32[1,264,128]{2,1,0:T(8,128)S(1)}, u32[]{:S(2)}, u32[]{:S(2)}) %collective-permute-start.7) | collective-permute-done | bytes 135200 | tf_op jit(solution)/shard_map/ppermute | solution.py:336
  37.3 1.4 %collective-permute-done.8 = f32[1,264,128]{2,1,0:T(8,128)S(1)} collective-permute-done((f32[1,264,128]{2,1,0:T(8,128)S(1)}, f32[1,264,128]{2,1,0:T(8,128)S(1)}, u32[]{:S(2)}, u32[]{:S(2)}) %collective-permute-start.8) | collective-permute-done | bytes 135200 | tf_op jit(solution)/shard_map/ppermute | solution.py:336
  38.8 0.2 shard_map.50.y_ref
  39.0 2.4 %collective-permute-start.9 = (f32[4,264,128]{2,1,0:T(8,128)S(1)}, f32[4,264,128]{2,1,0:T(8,128)S(1)}, u32[]{:S(2)}, u32[]{:S(2)}) collective-permute-start(f32[4,264,128]{2,1,0:T(8,128)S(1)} %pad_maximum_fusion.mine_ref), channel_id=1, source_target_pairs={{0,16},{1,17},{2,18},{3,19},{4,20},{5,21},{6,22},{7,23},{8,24},{9,... | collective-permute-start | bytes 1622024 | tf_op jit(solution)/shard_map/ppermute | solution.py:336
  41.4 0.1 collective-permute-start.10
  41.5 1.7 %collective-permute-done.10.y_other_ref = f32[64,512]{1,0:T(8,128)S(1)} collective-permute-done((f32[64,512]{1,0:T(8,128)S(1)}, f32[64,512]{1,0:T(8,128)S(1)}, u32[]{:S(2)}, u32[]{:S(2)}) %collective-permute-start.10) | collective-permute-done | bytes 131104 | tf_op jit(solution)/shard_map/ppermute | solution.py:336
  43.2 5.2 %shard_map.51 = (f32[64,1024]{1,0:T(8,128)}, f32[1,64]{1,0:T(1,128)}) custom-call(s32[1,1]{1,0:T(1,128)} %copy.11.valid_ref, f32[4,264,128]{2,1,0:T(8,128)S(1)} %pad_maximum_fusion.mine_ref, f32[4,264,128]{2,1,0:T(8,128)S(1)} %collective-permute-done.9.other_ref, f32[64,512]{1,0:T(8,128)S(1)} %shard_map.50.y_ref, ...), custom_call_target="tpu_custom_call" | custom-call | tf_op jit(solution)/shard_map/pallas_call | solution.py:409
  (21 shorter events, 0.4 us)
Async XLA Ops:
  4.4 7.1 %collective-permute-start.2 = (f32[1,264,128]{2,1,0:T(8,128)S(1)}, f32[1,264,128]{2,1,0:T(8,128)S(1)}, u32[]{:S(2)}, u32[]{:S(2)}) collective-permute-start(f32[1,264,128]{2,1,0:T(8,128)S(1)} %get-tuple-element.19), channel_id=1, source_target_pairs={{0,4},{1,5},{2,6},{3,7},{4,0},{5,1},{6,2},{7,3},{8,12},{9,13},{10,... | collective-permute-start | bytes 405512 | tf_op jit(solution)/shard_map/ppermute | solution.py:336
  8.5 5.0 %collective-permute-start.1 = (f32[1,264,128]{2,1,0:T(8,128)S(1)}, f32[1,264,128]{2,1,0:T(8,128)S(1)}, u32[]{:S(2)}, u32[]{:S(2)}) collective-permute-start(f32[1,264,128]{2,1,0:T(8,128)S(1)} %get-tuple-element.18), channel_id=1, source_target_pairs={{0,2},{1,3},{2,0},{3,1},{4,6},{5,7},{6,4},{7,5},{8,10},{9,11},{10,... | collective-permute-start | bytes 405512 | tf_op jit(solution)/shard_map/ppermute | solution.py:336
  10.1 6.8 %collective-permute-start = (f32[1,264,128]{2,1,0:T(8,128)S(1)}, f32[1,264,128]{2,1,0:T(8,128)S(1)}, u32[]{:S(2)}, u32[]{:S(2)}) collective-permute-start(f32[1,264,128]{2,1,0:T(8,128)S(1)} %get-tuple-element.17), channel_id=1, source_target_pairs={{0,6},{1,7},{2,4},{3,5},{4,2},{5,3},{6,0},{7,1},{8,14},{9,15},{10,... | collective-permute-start | bytes 405512 | tf_op jit(solution)/shard_map/ppermute | solution.py:336
  16.9 6.0 %collective-permute-start.5 = (f32[1,264,128]{2,1,0:T(8,128)S(1)}, f32[1,264,128]{2,1,0:T(8,128)S(1)}, u32[]{:S(2)}, u32[]{:S(2)}) collective-permute-start(f32[1,264,128]{2,1,0:T(8,128)S(1)} %fusion.9), channel_id=1, source_target_pairs={{0,9},{1,8},{2,11},{3,10},{4,13},{5,12},{6,15},{7,14},{8,1},{9,0},... | collective-permute-start | bytes 405512 | tf_op jit(solution)/shard_map/ppermute | solution.py:336
  19.5 5.0 %collective-permute-start.4 = (f32[1,264,128]{2,1,0:T(8,128)S(1)}, f32[1,264,128]{2,1,0:T(8,128)S(1)}, u32[]{:S(2)}, u32[]{:S(2)}) collective-permute-start(f32[1,264,128]{2,1,0:T(8,128)S(1)} %fusion.9), channel_id=1, source_target_pairs={{0,8},{1,9},{2,10},{3,11},{4,12},{5,13},{6,14},{7,15},{8,0},{9,1},... | collective-permute-start | bytes 405512 | tf_op jit(solution)/shard_map/ppermute | solution.py:336
  20.0 5.0 %collective-permute-start.3 = (f32[1,264,128]{2,1,0:T(8,128)S(1)}, f32[1,264,128]{2,1,0:T(8,128)S(1)}, u32[]{:S(2)}, u32[]{:S(2)}) collective-permute-start(f32[1,264,128]{2,1,0:T(8,128)S(1)} %fusion.9), channel_id=1, source_target_pairs={{0,1},{1,0},{2,3},{3,2},{4,5},{5,4},{6,7},{7,6},{8,9},{9,8},{10,11... | collective-permute-start | bytes 405512 | tf_op jit(solution)/shard_map/ppermute | solution.py:336
  25.1 8.2 %collective-permute-start.6 = (f32[1,264,128]{2,1,0:T(8,128)S(1)}, f32[1,264,128]{2,1,0:T(8,128)S(1)}, u32[]{:S(2)}, u32[]{:S(2)}) collective-permute-start(f32[1,264,128]{2,1,0:T(8,128)S(1)} %add_add_fusion), channel_id=1, source_target_pairs={{0,6},{1,7},{2,4},{3,5},{4,2},{5,3},{6,0},{7,1},{8,14},{9,15},{10,... | collective-permute-start | bytes 405512 | tf_op jit(solution)/shard_map/ppermute | solution.py:336
  26.6 10.7 %collective-permute-start.7 = (f32[1,264,128]{2,1,0:T(8,128)S(1)}, f32[1,264,128]{2,1,0:T(8,128)S(1)}, u32[]{:S(2)}, u32[]{:S(2)}) collective-permute-start(f32[1,264,128]{2,1,0:T(8,128)S(1)} %add_add_fusion), channel_id=1, source_target_pairs={{0,4},{1,5},{2,6},{3,7},{4,0},{5,1},{6,2},{7,3},{8,12},{9,13},{10,... | collective-permute-start | bytes 405512 | tf_op jit(solution)/shard_map/ppermute | solution.py:336
  32.8 5.8 %collective-permute-start.8 = (f32[1,264,128]{2,1,0:T(8,128)S(1)}, f32[1,264,128]{2,1,0:T(8,128)S(1)}, u32[]{:S(2)}, u32[]{:S(2)}) collective-permute-start(f32[1,264,128]{2,1,0:T(8,128)S(1)} %add_add_fusion), channel_id=1, source_target_pairs={{0,2},{1,3},{2,0},{3,1},{4,6},{5,7},{6,4},{7,5},{8,10},{9,11},{10,... | collective-permute-start | bytes 405512 | tf_op jit(solution)/shard_map/ppermute | solution.py:336
  38.7 4.4 %copy-start = (bf16[1,1024,512]{2,1,0:T(8,128)(2,1)S(1)}, bf16[1,1024,512]{2,1,0:T(8,128)(2,1)}, u32[]{:S(2)}) copy-start(bf16[1,1024,512]{2,1,0:T(8,128)(2,1)} %param.3) | copy-start | bytes 3145732
  39.0 4.2 %collective-permute-start.9 = (f32[4,264,128]{2,1,0:T(8,128)S(1)}, f32[4,264,128]{2,1,0:T(8,128)S(1)}, u32[]{:S(2)}, u32[]{:S(2)}) collective-permute-start(f32[4,264,128]{2,1,0:T(8,128)S(1)} %pad_maximum_fusion.mine_ref), channel_id=1, source_target_pairs={{0,16},{1,17},{2,18},{3,19},{4,20},{5,21},{6,22},{7,23},{8,24},{9,... | collective-permute-start | bytes 1622024 | tf_op jit(solution)/shard_map/ppermute | solution.py:336
  41.4 1.7 %collective-permute-start.10 = (f32[64,512]{1,0:T(8,128)S(1)}, f32[64,512]{1,0:T(8,128)S(1)}, u32[]{:S(2)}, u32[]{:S(2)}) collective-permute-start(f32[64,512]{1,0:T(8,128)S(1)} %shard_map.50.y_ref), channel_id=1, source_target_pairs={{0,16},{1,17},{2,18},{3,19},{4,20},{5,21},{6,22},{7,23},{8,24},{9,... | collective-permute-start | bytes 393224 | tf_op jit(solution)/shard_map/ppermute | solution.py:336

commit v5 on v4

--- a/solution.py
+++ b/solution.py
@@ -5,20 +5,14 @@
 from jax.experimental.pallas import tpu as pltpu
 from jax.sharding import PartitionSpec as P
 
-HIGH = lax.Precision.HIGHEST
 F32 = jnp.float32
 BLOCK = 128
 TILE = 8
 HALF = 64
+WIDE = 256
 GRANT = 16 * 2**20
 VMEM = pl.BlockSpec(memory_space=pltpu.VMEM)
 SMEM = pl.BlockSpec(memory_space=pltpu.SMEM)
-
-
-def dot(a, b, ca=1, cb=0):
-    return lax.dot_general(
-        a, b, (((ca,), (cb,)), ((), ())), precision=HIGH, preferred_element_type=F32
-    )
 
 
 def thirds(x):
@@ -52,6 +46,15 @@
     rows = a.shape[0]
     both = plain(jnp.concatenate([ah, am], axis=0), bh)
     return both[:rows] + (both[rows:] + plain(ah, bm))
+
+
+def rows_product(a, b):
+    ah, am, al = thirds(a)
+    bh, bm, bl = thirds(b)
+    m = a.shape[0]
+    p = plain(jnp.concatenate([ah, am, al], axis=0), bh, 1, 1)
+    q = plain(jnp.concatenate([ah, am], axis=0), bm, 1, 1)
+    return p[:m] + ((p[m : 2 * m] + q[:m]) + (p[2 * m :] + q[m:] + plain(ah, bl, 1, 1)))
 
 
 def lane_copy(tile, lane):
@@ -143,26 +146,35 @@
     return shared + [(i, j) for i in range(nb) for j in range(i + 1, nb)]
 
 
-def pack(gram, count):
-    nb = gram.shape[0] // BLOCK
-
-    def block(i, j):
-        return gram[i * BLOCK : (i + 1) * BLOCK, j * BLOCK : (j + 1) * BLOCK]
-
+def gram_kernel(valid_ref, values_hbm, out_ref, values_ref, gram_ref, sem):
+    copy = pltpu.make_async_copy(values_hbm, values_ref, sem)
+    copy.start()
+    points, n = values_ref.shape
+    nb = n // BLOCK
+    ocean = valid_ref[0, 0]
+    place, _ = iotas((points, n))
+    copy.wait()
+    masked = jnp.where(place < ocean, values_ref[...].astype(F32), 0.0).astype(jnp.bfloat16)
+    for start in range(0, n, WIDE):
+        stop = min(start + WIDE, n)
+        gram_ref[start:stop, start:] = plain(masked[:, start:stop], masked[:, start:], 0, 0)
     row, lane = iotas((BLOCK, BLOCK))
-    parts, extra = [], [jnp.full((1, BLOCK), count, F32)]
-    for i, j in layout(nb):
+    quarter = nb * nb * BLOCK // 8
+    extra = [jnp.full((1, BLOCK), ocean.astype(F32))]
+    for t, (i, j) in enumerate(layout(nb)):
+        block = gram_ref[span(i), span(j)]
         if i == j:
-            second = block(i + 1, i + 1)
-            parts.append(jnp.where(row <= lane, block(i, i), second))
+            second = gram_ref[span(i + 1), span(i + 1)]
+            block = jnp.where(row <= lane, block, second)
             extra.append(jnp.sum(jnp.where(row == lane, second, 0.0), axis=0, keepdims=True))
-        else:
-            parts.append(block(i, j))
+        half = BLOCK // 2
+        for h in range(2):
+            part, offset = divmod(t * BLOCK + half * h, quarter)
+            out_ref[part, offset : offset + half, :] = block[half * h : half * (h + 1)]
     fill = jnp.zeros((-len(extra) % TILE, BLOCK), F32)
     extra = jnp.concatenate(extra + [fill], axis=0)
-    parts = jnp.concatenate(parts, axis=0)
-    parts = parts.reshape(4, parts.shape[0] // 4, BLOCK)
-    return jnp.concatenate([parts, jnp.broadcast_to(extra, (4,) + extra.shape)], axis=1)
+    for part in range(4):
+        out_ref[part, quarter:, :] = extra
 
 
 def unpack(read, nb, put):
@@ -288,13 +300,13 @@
     y = jnp.where(first, y_other_ref[...], y_ref[...])
     fill(0)
     t = two_thirds(y, g_ref[0])
-    product = dot(y, t, 1, 1)
+    product = rows_product(y, t)
     fill(1)
     inverse = normal(product)
     q0 = two_thirds(inverse, y)
     z = two_thirds(inverse, t)
     w = two_thirds(z, g_ref[1])
-    inverse = normal(dot(z, w, 1, 1))
+    inverse = normal(rows_product(z, w))
     q1 = two_thirds(inverse, z)
     row, lane = iotas((modes, modes))
     diagonal = jnp.sum(jnp.where(row == lane, inverse, 0.0), axis=0, keepdims=True)
@@ -383,13 +395,21 @@
     values = anomalies[0]
     rows_here, n = values.shape
     modes = start_basis.shape[1]
-    ocean = valid_rows[0, 0]
-    place = lax.broadcasted_iota(jnp.int32, (rows_here, 1), 0)
-    masked = jnp.where(place < ocean, values, jnp.zeros_like(values))
-    gram = lax.dot_general(
-        masked, masked, (((0,), (0,)), ((), ())), preferred_element_type=F32
-    )
-    mine = sum_all(pack(gram, ocean.astype(F32)))
+    nb = n // BLOCK
+    extra = -(-(1 + nb // 2) // TILE) * TILE
+    packed = pl.pallas_call(
+        gram_kernel,
+        out_shape=jax.ShapeDtypeStruct((4, nb * nb * BLOCK // 8 + extra, BLOCK), F32),
+        in_specs=[SMEM, pl.BlockSpec(memory_space=pltpu.HBM)],
+        out_specs=VMEM,
+        scratch_shapes=[
+            pltpu.VMEM((rows_here, n), jnp.bfloat16),
+            pltpu.VMEM((n, n), F32),
+            pltpu.SemaphoreType.DMA,
+        ],
+        compiler_params=pltpu.CompilerParams(vmem_limit_bytes=GRANT),
+    )(valid_rows, pltpu.with_memory_space_constraint(values, pltpu.HBM))
+    mine = sum_all(packed)
     y = pl.pallas_call(
         factor_kernel,
         out_shape=jax.ShapeDtypeStruct((modes, n), F32),

time: 48.7 us -> 48.9 us (level)
  matrix products: 2.68 us -> 0 us
  Pallas kernels: 5.39 us -> 7.26 us
  waiting for transfers between devices: 18.4 us -> 19.3 us
    dot_general x1 -> x0, matrix products: 2.68 us -> none  [per_device(): lax.dot_general(masked, masked, (((0,), (0,)), ((), ())), preferred_eleme...]
    pallas_call x0 -> x1, Pallas kernels: none -> 1.93 us  [per_device(): pl.pallas_call(gram_kernel, out_shape=jax.ShapeDtypeStruct((4, nb * nb *...]
    ppermute x11, waiting for transfers between devices: 18.4 us -> 19.3 us  [swap(): return lax.ppermute(value, AXES, moves)]
  transfers between devices with their start and end apart: 11 -> 11, of which waited for: 9 -> 7; matrix products, arithmetic and copies ran while one was open for 0% -> 0% of each run, Pallas kernels for 0% -> 0%
where the time goes in v5:
time: 48.9 us; the launch traced here: 48.7 us
  starting transfers between devices  20.4 us (42%)
  waiting for transfers between devices  19.3 us (39%)
  Pallas kernels  7.26 us (15%)
  between operations  1.53 us (3%)
    ppermute x11, starting transfers between devices, swap(): return lax.ppermute(value, AXES, moves)  20.4 us
    ppermute x11, waiting for transfers between devices, swap(): return lax.ppermute(value, AXES, moves)  19.3 us
    pallas_call x1, Pallas kernels, per_device(): pl.pallas_call(finish_kernel, out_shape=(jax.ShapeDtypeStruct((modes, row...  5.11 us
    pallas_call x1, Pallas kernels, per_device(): pl.pallas_call(gram_kernel, out_shape=jax.ShapeDtypeStruct((4, nb * nb *...  1.93 us
  transfers between devices with their start and end apart: 11, of which 7 were waited for; matrix products, arithmetic and copies ran while one was open for 0% of the time, Pallas kernels for 0%

profile of v5, /device:TPU:0, one launch (start us, length us, event | category | flops | bytes accessed | tf_op | source)
XLA Modules:
  0.0 48.7 jit_solution(4350058198214684620)
XLA Ops:
  1.3 1.9 %shard_map.50 = f32[4,264,128]{2,1,0:T(8,128)S(1)} custom-call(s32[1,1]{1,0:T(1,128)S(6)} %copy.5.valid_ref, bf16[1024,512]{1,0:T(8,128)(2,1)} %bitcast.6), custom_call_target="tpu_custom_call" | custom-call | tf_op jit(solution)/shard_map/pallas_call | solution.py:400
  3.3 5.1 %collective-permute-start = (f32[1,264,128]{2,1,0:T(8,128)S(1)}, f32[1,264,128]{2,1,0:T(8,128)S(1)}, u32[]{:S(2)}, u32[]{:S(2)}) collective-permute-start(f32[1,264,128]{2,1,0:T(8,128)S(1)} %get-tuple-element.14), channel_id=1, source_target_pairs={{0,6},{1,7},{2,4},{3,5},{4,2},{5,3},{6,0},{7,1},{8,14},{9,15},{10,... | collective-permute-start | bytes 405512 | tf_op jit(solution)/shard_map/ppermute | solution.py:348
  8.4 0.0 collective-permute-start.2
  8.4 0.6 %collective-permute-start.1 = (f32[1,264,128]{2,1,0:T(8,128)S(1)}, f32[1,264,128]{2,1,0:T(8,128)S(1)}, u32[]{:S(2)}, u32[]{:S(2)}) collective-permute-start(f32[1,264,128]{2,1,0:T(8,128)S(1)} %get-tuple-element.16), channel_id=1, source_target_pairs={{0,2},{1,3},{2,0},{3,1},{4,6},{5,7},{6,4},{7,5},{8,10},{9,11},{10,... | collective-permute-start | bytes 405512 | tf_op jit(solution)/shard_map/ppermute | solution.py:348
  9.1 2.4 %collective-permute-done = f32[1,264,128]{2,1,0:T(8,128)S(1)} collective-permute-done((f32[1,264,128]{2,1,0:T(8,128)S(1)}, f32[1,264,128]{2,1,0:T(8,128)S(1)}, u32[]{:S(2)}, u32[]{:S(2)}) %collective-permute-start) | collective-permute-done | bytes 135200 | tf_op jit(solution)/shard_map/ppermute | solution.py:348
  11.5 3.9 %collective-permute-done.2 = f32[1,264,128]{2,1,0:T(8,128)S(1)} collective-permute-done((f32[1,264,128]{2,1,0:T(8,128)S(1)}, f32[1,264,128]{2,1,0:T(8,128)S(1)}, u32[]{:S(2)}, u32[]{:S(2)}) %collective-permute-start.2) | collective-permute-done | bytes 135200 | tf_op jit(solution)/shard_map/ppermute | solution.py:348
  15.5 0.0 collective-permute-done.1
  15.5 6.2 %collective-permute-start.5 = (f32[1,264,128]{2,1,0:T(8,128)S(1)}, f32[1,264,128]{2,1,0:T(8,128)S(1)}, u32[]{:S(2)}, u32[]{:S(2)}) collective-permute-start(f32[1,264,128]{2,1,0:T(8,128)S(1)} %add_add_fusion.1), channel_id=1, source_target_pairs={{0,9},{1,8},{2,11},{3,10},{4,13},{5,12},{6,15},{7,14},{8,1},{9,0},... | collective-permute-start | bytes 405512 | tf_op jit(solution)/shard_map/ppermute | solution.py:348
  21.7 0.0 collective-permute-start.4
  21.7 0.6 %collective-permute-start.3 = (f32[1,264,128]{2,1,0:T(8,128)S(1)}, f32[1,264,128]{2,1,0:T(8,128)S(1)}, u32[]{:S(2)}, u32[]{:S(2)}) collective-permute-start(f32[1,264,128]{2,1,0:T(8,128)S(1)} %add_add_fusion.1), channel_id=1, source_target_pairs={{0,1},{1,0},{2,3},{3,2},{4,5},{5,4},{6,7},{7,6},{8,9},{9,8},{10,11... | collective-permute-start | bytes 405512 | tf_op jit(solution)/shard_map/ppermute | solution.py:348
  22.3 3.3 %collective-permute-done.5 = f32[1,264,128]{2,1,0:T(8,128)S(1)} collective-permute-done((f32[1,264,128]{2,1,0:T(8,128)S(1)}, f32[1,264,128]{2,1,0:T(8,128)S(1)}, u32[]{:S(2)}, u32[]{:S(2)}) %collective-permute-start.5) | collective-permute-done | bytes 135200 | tf_op jit(solution)/shard_map/ppermute | solution.py:348
  25.6 3.4 %collective-permute-done.4 = f32[1,264,128]{2,1,0:T(8,128)S(1)} collective-permute-done((f32[1,264,128]{2,1,0:T(8,128)S(1)}, f32[1,264,128]{2,1,0:T(8,128)S(1)}, u32[]{:S(2)}, u32[]{:S(2)}) %collective-permute-start.4) | collective-permute-done | bytes 135200 | tf_op jit(solution)/shard_map/ppermute | solution.py:348
  29.0 0.1 collective-permute-start.8
  29.1 0.1 collective-permute-start.7
  29.2 4.3 %collective-permute-start.6 = (f32[1,264,128]{2,1,0:T(8,128)S(1)}, f32[1,264,128]{2,1,0:T(8,128)S(1)}, u32[]{:S(2)}, u32[]{:S(2)}) collective-permute-start(f32[1,264,128]{2,1,0:T(8,128)S(1)} %add_add_fusion), channel_id=1, source_target_pairs={{0,6},{1,7},{2,4},{3,5},{4,2},{5,3},{6,0},{7,1},{8,14},{9,15},{10,... | collective-permute-start | bytes 405512 | tf_op jit(solution)/shard_map/ppermute | solution.py:348
  33.5 2.1 %collective-permute-done.8 = f32[1,264,128]{2,1,0:T(8,128)S(1)} collective-permute-done((f32[1,264,128]{2,1,0:T(8,128)S(1)}, f32[1,264,128]{2,1,0:T(8,128)S(1)}, u32[]{:S(2)}, u32[]{:S(2)}) %collective-permute-start.8) | collective-permute-done | bytes 135200 | tf_op jit(solution)/shard_map/ppermute | solution.py:348
  35.5 2.5 %collective-permute-done.7 = f32[1,264,128]{2,1,0:T(8,128)S(1)} collective-permute-done((f32[1,264,128]{2,1,0:T(8,128)S(1)}, f32[1,264,128]{2,1,0:T(8,128)S(1)}, u32[]{:S(2)}, u32[]{:S(2)}) %collective-permute-start.7) | collective-permute-done | bytes 135200 | tf_op jit(solution)/shard_map/ppermute | solution.py:348
  38.0 0.1 select_select_fusion.3
  38.1 0.0 copy-start
  38.2 0.2 shard_map.51.y_ref
  38.4 3.3 %collective-permute-start.9 = (f32[4,264,128]{2,1,0:T(8,128)S(1)}, f32[4,264,128]{2,1,0:T(8,128)S(1)}, u32[]{:S(2)}, u32[]{:S(2)}) collective-permute-start(f32[4,264,128]{2,1,0:T(8,128)S(1)} %pad_maximum_fusion.mine_ref), channel_id=1, source_target_pairs={{0,16},{1,17},{2,18},{3,19},{4,20},{5,21},{6,22},{7,23},{8,24},{9,... | collective-permute-start | bytes 1622024 | tf_op jit(solution)/shard_map/ppermute | solution.py:348
  41.7 0.1 collective-permute-start.10
  41.7 1.7 %collective-permute-done.10.y_other_ref = f32[64,512]{1,0:T(8,128)S(1)} collective-permute-done((f32[64,512]{1,0:T(8,128)S(1)}, f32[64,512]{1,0:T(8,128)S(1)}, u32[]{:S(2)}, u32[]{:S(2)}) %collective-permute-start.10) | collective-permute-done | bytes 131104 | tf_op jit(solution)/shard_map/ppermute | solution.py:348
  43.4 5.1 %shard_map.52 = (f32[64,1024]{1,0:T(8,128)}, f32[1,64]{1,0:T(1,128)}) custom-call(s32[1,1]{1,0:T(1,128)S(6)} %copy.5.valid_ref, f32[4,264,128]{2,1,0:T(8,128)S(1)} %pad_maximum_fusion.mine_ref, f32[4,264,128]{2,1,0:T(8,128)S(1)} %collective-permute-done.9.other_ref, f32[64,512]{1,0:T(8,128)S(1)} %shard_map.51.y_ref, ...), custom_call_target="tpu_custom_call" | custom-call | tf_op jit(solution)/shard_map/pallas_call | solution.py:429
  (8 shorter events, 0.2 us)
Async XLA Ops:
  3.3 8.2 %collective-permute-start = (f32[1,264,128]{2,1,0:T(8,128)S(1)}, f32[1,264,128]{2,1,0:T(8,128)S(1)}, u32[]{:S(2)}, u32[]{:S(2)}) collective-permute-start(f32[1,264,128]{2,1,0:T(8,128)S(1)} %get-tuple-element.14), channel_id=1, source_target_pairs={{0,6},{1,7},{2,4},{3,5},{4,2},{5,3},{6,0},{7,1},{8,14},{9,15},{10,... | collective-permute-start | bytes 405512 | tf_op jit(solution)/shard_map/ppermute | solution.py:348
  8.4 7.0 %collective-permute-start.2 = (f32[1,264,128]{2,1,0:T(8,128)S(1)}, f32[1,264,128]{2,1,0:T(8,128)S(1)}, u32[]{:S(2)}, u32[]{:S(2)}) collective-permute-start(f32[1,264,128]{2,1,0:T(8,128)S(1)} %get-tuple-element.15), channel_id=1, source_target_pairs={{0,4},{1,5},{2,6},{3,7},{4,0},{5,1},{6,2},{7,3},{8,12},{9,13},{10,... | collective-permute-start | bytes 405512 | tf_op jit(solution)/shard_map/ppermute | solution.py:348
  8.4 7.0 %collective-permute-start.1 = (f32[1,264,128]{2,1,0:T(8,128)S(1)}, f32[1,264,128]{2,1,0:T(8,128)S(1)}, u32[]{:S(2)}, u32[]{:S(2)}) collective-permute-start(f32[1,264,128]{2,1,0:T(8,128)S(1)} %get-tuple-element.16), channel_id=1, source_target_pairs={{0,2},{1,3},{2,0},{3,1},{4,6},{5,7},{6,4},{7,5},{8,10},{9,11},{10,... | collective-permute-start | bytes 405512 | tf_op jit(solution)/shard_map/ppermute | solution.py:348
  15.5 10.1 %collective-permute-start.5 = (f32[1,264,128]{2,1,0:T(8,128)S(1)}, f32[1,264,128]{2,1,0:T(8,128)S(1)}, u32[]{:S(2)}, u32[]{:S(2)}) collective-permute-start(f32[1,264,128]{2,1,0:T(8,128)S(1)} %add_add_fusion.1), channel_id=1, source_target_pairs={{0,9},{1,8},{2,11},{3,10},{4,13},{5,12},{6,15},{7,14},{8,1},{9,0},... | collective-permute-start | bytes 405512 | tf_op jit(solution)/shard_map/ppermute | solution.py:348
  21.7 7.3 %collective-permute-start.4 = (f32[1,264,128]{2,1,0:T(8,128)S(1)}, f32[1,264,128]{2,1,0:T(8,128)S(1)}, u32[]{:S(2)}, u32[]{:S(2)}) collective-permute-start(f32[1,264,128]{2,1,0:T(8,128)S(1)} %add_add_fusion.1), channel_id=1, source_target_pairs={{0,8},{1,9},{2,10},{3,11},{4,12},{5,13},{6,14},{7,15},{8,0},{9,1},... | collective-permute-start | bytes 405512 | tf_op jit(solution)/shard_map/ppermute | solution.py:348
  21.7 7.3 %collective-permute-start.3 = (f32[1,264,128]{2,1,0:T(8,128)S(1)}, f32[1,264,128]{2,1,0:T(8,128)S(1)}, u32[]{:S(2)}, u32[]{:S(2)}) collective-permute-start(f32[1,264,128]{2,1,0:T(8,128)S(1)} %add_add_fusion.1), channel_id=1, source_target_pairs={{0,1},{1,0},{2,3},{3,2},{4,5},{5,4},{6,7},{7,6},{8,9},{9,8},{10,11... | collective-permute-start | bytes 405512 | tf_op jit(solution)/shard_map/ppermute | solution.py:348
  29.0 6.5 %collective-permute-start.8 = (f32[1,264,128]{2,1,0:T(8,128)S(1)}, f32[1,264,128]{2,1,0:T(8,128)S(1)}, u32[]{:S(2)}, u32[]{:S(2)}) collective-permute-start(f32[1,264,128]{2,1,0:T(8,128)S(1)} %add_add_fusion), channel_id=1, source_target_pairs={{0,2},{1,3},{2,0},{3,1},{4,6},{5,7},{6,4},{7,5},{8,10},{9,11},{10,... | collective-permute-start | bytes 405512 | tf_op jit(solution)/shard_map/ppermute | solution.py:348
  29.1 8.9 %collective-permute-start.7 = (f32[1,264,128]{2,1,0:T(8,128)S(1)}, f32[1,264,128]{2,1,0:T(8,128)S(1)}, u32[]{:S(2)}, u32[]{:S(2)}) collective-permute-start(f32[1,264,128]{2,1,0:T(8,128)S(1)} %add_add_fusion), channel_id=1, source_target_pairs={{0,4},{1,5},{2,6},{3,7},{4,0},{5,1},{6,2},{7,3},{8,12},{9,13},{10,... | collective-permute-start | bytes 405512 | tf_op jit(solution)/shard_map/ppermute | solution.py:348
  29.2 8.8 %collective-permute-start.6 = (f32[1,264,128]{2,1,0:T(8,128)S(1)}, f32[1,264,128]{2,1,0:T(8,128)S(1)}, u32[]{:S(2)}, u32[]{:S(2)}) collective-permute-start(f32[1,264,128]{2,1,0:T(8,128)S(1)} %add_add_fusion), channel_id=1, source_target_pairs={{0,6},{1,7},{2,4},{3,5},{4,2},{5,3},{6,0},{7,1},{8,14},{9,15},{10,... | collective-permute-start | bytes 405512 | tf_op jit(solution)/shard_map/ppermute | solution.py:348
  38.1 5.3 %copy-start = (bf16[1,1024,512]{2,1,0:T(8,128)(2,1)S(1)}, bf16[1,1024,512]{2,1,0:T(8,128)(2,1)}, u32[]{:S(2)}) copy-start(bf16[1,1024,512]{2,1,0:T(8,128)(2,1)} %param.3) | copy-start | bytes 3145732
  38.4 5.0 %collective-permute-start.9 = (f32[4,264,128]{2,1,0:T(8,128)S(1)}, f32[4,264,128]{2,1,0:T(8,128)S(1)}, u32[]{:S(2)}, u32[]{:S(2)}) collective-permute-start(f32[4,264,128]{2,1,0:T(8,128)S(1)} %pad_maximum_fusion.mine_ref), channel_id=1, source_target_pairs={{0,16},{1,17},{2,18},{3,19},{4,20},{5,21},{6,22},{7,23},{8,24},{9,... | collective-permute-start | bytes 1622024 | tf_op jit(solution)/shard_map/ppermute | solution.py:348
  41.7 1.7 %collective-permute-start.10 = (f32[64,512]{1,0:T(8,128)S(1)}, f32[64,512]{1,0:T(8,128)S(1)}, u32[]{:S(2)}, u32[]{:S(2)}) collective-permute-start(f32[64,512]{1,0:T(8,128)S(1)} %shard_map.51.y_ref), channel_id=1, source_target_pairs={{0,16},{1,17},{2,18},{3,19},{4,20},{5,21},{6,22},{7,23},{8,24},{9,... | collective-permute-start | bytes 393224 | tf_op jit(solution)/shard_map/ppermute | solution.py:348
